TPU v7x, 768 devices: a whole 4x8x12 slice. The times are simulated.
768 devices in a mesh: sect: 3 (over z_hi), lon: 32 (over x, z_lo, core), lat: 8 (over y).
Axes of the slice: x: 4, y: 8, z: 12 (z_hi: 3, z_lo: 4; z = z_hi * 4 + z_lo), core: 2. Of those that a mesh axis runs over, the one named last changes fastest.
Arguments:
- fields: float32 [3, 6, 16, 64, 4096], P('sect', None, None, 'lat', 'lon'), may hold values from -3 to 3, as said below
- levels: int32 [64, 4096], P('lat', 'lon'), may hold values from 0 to 16, as said below
Outputs:
- new_fields: float32 [3, 6, 16, 64, 4096], P('sect', None, None, 'lat', 'lon')
Inputs may be any that keep to these rules, and one draw needn't show every extreme that they name: `fields`: section 0: velocities of magnitude below 0.95, temperature and salinity, lateral viscosity between 0.02 and 0.2, background diffusivity between 0.05 and 2. Later sections: tracers. In each device's block of 8 x 128 columns at most 768 columns have levels above 0, and some block has exactly 768; the value 16 occurs in every draw.
All inputs are finite; a program needn't handle non-finite values.
Results may differ from a plain program's by a relative error of at most 0.00002.
Values sent between devices are 32-bit elements; how exact they have to be, the bound alone decides.
A program may use at most 32 MiB of HBM per device.

v0:
```python
import jax
import jax.numpy as jnp
from jax import lax
from jax.sharding import PartitionSpec as P

NSUB = 2


TIME_STEP = 1.0
CORIOLIS = 0.3
THERMAL = 0.2
HALINE = 0.15
GRAVITY_SCALE = 0.05
MIX_BOOST = 4.0
RICHARDSON = 1.0


def padded(shard, sides, width):
    edges = {}
    for axis, dim in sides:
        size, length = (lax.axis_size(axis), shard.shape[dim])
        up = [(i, (i + 1) % size) for i in range(size)]
        last = lax.slice_in_dim(shard, length - width, length, axis=dim)
        initial = lax.slice_in_dim(shard, 0, width, axis=dim)
        edges[dim] = (
            lax.ppermute(last, axis, up),
            lax.ppermute(initial, axis, [(b, a) for a, b in up]),
        )
    done = []
    for _, dim in sides:
        low, high = edges[dim]
        around = [(width, width) if d in done else (0, 0) for d in range(shard.ndim)]
        shard = jnp.concatenate([jnp.pad(low, around), shard, jnp.pad(high, around)], axis=dim)
        done.append(dim)
    return shard


def picked(shard, axis, root):
    return lax.dynamic_index_in_dim(lax.all_gather(shard, axis), root, 0, keepdims=False)


def with_halo(cells, sides, width):
    for axis, dim in sides:
        count = lax.axis_size(axis)
        head = lax.slice_in_dim(cells, 0, width, axis=dim)
        tail = lax.slice_in_dim(cells, cells.shape[dim] - width, cells.shape[dim], axis=dim)
        cells = jnp.concatenate(
            [
                lax.ppermute(tail, axis, [(i, (i + 1) % count) for i in range(count)]),
                cells,
                lax.ppermute(head, axis, [((i + 1) % count, i) for i in range(count)]),
            ],
            axis=dim,
        )
    return cells


def centre(extended):
    return extended[..., 1:-1, 1:-1]


def to_east(extended):
    return extended[..., 1:-1, 2:]


def to_west(extended):
    return extended[..., 1:-1, :-2]


def to_north(extended):
    return extended[..., 2:, 1:-1]


def to_south(extended):
    return extended[..., :-2, 1:-1]


def clear_edges(extended, rim_width):
    row_total = extended.shape[-2]
    row_ids = lax.broadcasted_iota(jnp.int32, (row_total, 1), 0)
    position = lax.axis_index("lat")
    lat_total = lax.axis_size("lat")
    low_bad = (position == 0) & (row_ids < rim_width)
    high_bad = (position == lat_total - 1) & (row_ids >= row_total - rim_width)
    return jnp.where(low_bad | high_bad, 0.0, extended)


def physics(extended, background):
    zonal_vel, merid_vel, temper, saline, viscosity, wetness = extended
    wet_mid = centre(wetness)
    mask_east = wet_mid * to_east(wetness)
    mask_west = to_west(wetness) * wet_mid
    mask_north = wet_mid * to_north(wetness)
    mask_south = to_south(wetness) * wet_mid
    flow_east = centre(zonal_vel) * mask_east
    flow_west = to_west(zonal_vel) * mask_west
    flow_north = centre(merid_vel) * mask_north
    flow_south = to_south(merid_vel) * mask_south
    divergence = flow_east - flow_west + (flow_north - flow_south)
    column_sum = jnp.cumsum(divergence[::-1], axis=0)[::-1]
    vertical = jnp.concatenate([jnp.zeros_like(column_sum[:1]), -column_sum[1:]], axis=0)
    visc_mid = centre(viscosity)
    coef_east = 0.5 * (visc_mid + to_east(viscosity)) * mask_east
    coef_west = 0.5 * (to_west(viscosity) + visc_mid) * mask_west
    coef_north = 0.5 * (visc_mid + to_north(viscosity)) * mask_north
    coef_south = 0.5 * (to_south(viscosity) + visc_mid) * mask_south

    def diffuse(quantity):
        middle = centre(quantity)
        return (
            coef_east * (to_east(quantity) - middle)
            - coef_west * (middle - to_west(quantity))
            + coef_north * (to_north(quantity) - middle)
            - coef_south * (middle - to_south(quantity))
        )

    density = HALINE * saline - THERMAL * temper
    pressure = GRAVITY_SCALE * jnp.cumsum(density * wetness, axis=0)
    press_mid = centre(pressure)
    zonal_new = (
        centre(zonal_vel)
        + TIME_STEP
        * (diffuse(zonal_vel) + CORIOLIS * centre(merid_vel) - (to_east(pressure) - press_mid))
    ) * mask_east
    merid_new = (
        centre(merid_vel)
        + TIME_STEP
        * (diffuse(merid_vel) - CORIOLIS * centre(zonal_vel) - (to_north(pressure) - press_mid))
    ) * mask_north
    temper_new = centre(temper) + TIME_STEP * diffuse(temper)
    saline_new = centre(saline) + TIME_STEP * diffuse(saline)
    temp_jump = THERMAL * (temper_new[:-1] - temper_new[1:])
    mixing = (
        background[1:]
        * (1.0 + MIX_BOOST / (1.0 + RICHARDSON * temp_jump * temp_jump))
        * wet_mid[1:]
    )
    diffusivity = jnp.concatenate([jnp.zeros_like(mixing[:1]), mixing], axis=0)
    return (
        (zonal_new, merid_new, temper_new, saline_new, vertical, diffusivity),
        (flow_east, flow_north, vertical, diffusivity),
    )


def advect(tracer_ext, east_ext, north_ext, step_size):
    east_mid = centre(east_ext)
    east_side = to_west(east_ext)
    north_mid = centre(north_ext)
    north_side = to_south(north_ext)
    middle = centre(tracer_ext)
    flux_east = jnp.maximum(east_mid, 0.0) * middle + jnp.minimum(east_mid, 0.0) * to_east(
        tracer_ext
    )
    flux_west = (
        jnp.maximum(east_side, 0.0) * to_west(tracer_ext) + jnp.minimum(east_side, 0.0) * middle
    )
    flux_north = jnp.maximum(north_mid, 0.0) * middle + jnp.minimum(north_mid, 0.0) * to_north(
        tracer_ext
    )
    flux_south = (
        jnp.maximum(north_side, 0.0) * to_south(tracer_ext) + jnp.minimum(north_side, 0.0) * middle
    )
    return middle - step_size * (flux_east - flux_west + (flux_north - flux_south))


def vertical_factor(vertical, diffusivity):
    up_part = jnp.maximum(vertical, 0.0) + diffusivity
    down_part = jnp.minimum(vertical, 0.0) - diffusivity
    zero_row = jnp.zeros_like(up_part[:1])
    up_next = jnp.concatenate([up_part[1:], zero_row], axis=0)
    down_next = jnp.concatenate([down_part[1:], zero_row], axis=0)
    lower_band = TIME_STEP * down_part
    diagonal = 1.0 + TIME_STEP * (up_part - down_next)
    upper_band = -TIME_STEP * up_next
    ratios = []
    inverses = []
    for index_k in range(vertical.shape[0]):
        pivot_value = diagonal[index_k]
        if index_k > 0:
            pivot_value = pivot_value - lower_band[index_k] * ratios[-1]
        inverse = 1.0 / pivot_value
        ratios.append(upper_band[index_k] * inverse)
        inverses.append(inverse)
    return (lower_band, ratios, inverses)


def thomas_solve(lower_band, ratios, inverses, rhs):
    level_count = rhs.shape[-2]
    forward = [rhs[..., 0, :] * inverses[0]]
    for index_k in range(1, level_count):
        forward.append(
            (rhs[..., index_k, :] - lower_band[index_k] * forward[-1]) * inverses[index_k]
        )
    result = [forward[-1]]
    for index_k in range(level_count - 2, -1, -1):
        result.append(forward[index_k] - ratios[index_k] * result[-1])
    return jnp.stack(result[::-1], axis=-2)


def on_device(fields, levels):
    own_slot = fields[0]
    field_count = own_slot.shape[0]
    layers = own_slot.shape[1]
    lat_rows = levels.shape[0]
    lon_cols = levels.shape[1]
    depth_ids = lax.broadcasted_iota(jnp.int32, (layers, lat_rows, lon_cols), 0)
    wetness = (depth_ids < levels[None]).astype(jnp.float32)
    dyn_ext = padded(
        jnp.concatenate([own_slot[:5], wetness[None]], axis=0), (("lon", 3), ("lat", 2)), 1
    )
    dyn_ext = clear_edges(dyn_ext, 1)
    outputs, flow_parts = physics(dyn_ext, own_slot[5])
    flow_stack = picked(jnp.stack(flow_parts), "sect", 0)
    sub_step = TIME_STEP / NSUB
    moving = jnp.concatenate([own_slot, flow_stack[0:2]], axis=0)
    extended = clear_edges(with_halo(moving, (("lon", 3), ("lat", 2)), NSUB), NSUB)
    tracer_ext = extended[:field_count]
    east_ext = extended[field_count]
    north_ext = extended[field_count + 1]
    current = tracer_ext
    for substep in range(NSUB):
        current = advect(current, east_ext, north_ext, sub_step)
        east_ext = centre(east_ext)
        north_ext = centre(north_ext)
    total_cols = lat_rows * lon_cols
    vert_flat = flow_stack[2].reshape(layers, total_cols)
    kappa_flat = flow_stack[3].reshape(layers, total_cols)
    flat_rhs = current.reshape(field_count, layers, total_cols)
    lower_band, ratios, inverses = vertical_factor(vert_flat, kappa_flat)
    solved = thomas_solve(lower_band, ratios, inverses, flat_rhs)
    tracer_out = solved.reshape(current.shape) * wetness
    is_physics = lax.axis_index("sect") == 0
    return jnp.where(is_physics, jnp.stack(outputs), tracer_out)[None]


def solution(mesh):
    return jax.shard_map(
        on_device,
        mesh=mesh,
        in_specs=(P("sect", None, None, "lat", "lon"), P("lat", "lon")),
        out_specs=P("sect", None, None, "lat", "lon"),
        check_vma=False,
    )
```

profile of v0, /device:TPU:6, one launch (start us, length us, event | category | flops | bytes accessed | tf_op | source)
XLA Modules:
  0.0 108.3 jit_solution(13089742529595128811)
XLA Ops:
  0.0 0.8 fusion.78
  0.8 1.0 slice_bitcast_fusion
  1.8 5.4 %collective-permute-start.3 = (f32[6,16,1,128]{3,2,1,0:T(1,128)S(1)}, f32[6,16,1,128]{3,2,1,0:T(1,128)S(1)}, u32[]{:S(2)}, u32[]{:S(2)}) collective-permute-start(f32[6,16,1,128]{3,2,1,0:T(1,128)S(1)} %get-tuple-element.87), channel_id=1, source_target_pairs={{1,0},{2,1},{3,2},{4,3},{5,4},{6,5},{7,6},{0,7},{9,8},{10,9},{11,1... | collective-permute-start | bytes 147464 | tf_op jit(solution)/shard_map/ppermute | solution.py:27
  7.2 1.9 %collective-permute-start = (f32[6,16,1,128]{3,2,1,0:T(1,128)S(1)}, f32[6,16,1,128]{3,2,1,0:T(1,128)S(1)}, u32[]{:S(2)}, u32[]{:S(2)}) collective-permute-start(f32[6,16,1,128]{3,2,1,0:T(1,128)S(1)} %get-tuple-element.86), channel_id=1, source_target_pairs={{0,1},{1,2},{2,3},{3,4},{4,5},{5,6},{6,7},{7,0},{8,9},{9,10},{10,1... | collective-permute-start | bytes 147464 | tf_op jit(solution)/shard_map/ppermute | solution.py:26
  9.3 7.3 %collective-permute-start.2 = (f32[6,16,8,1]{3,2,1,0:T(8,128)S(1)}, f32[6,16,8,1]{3,2,1,0:T(8,128)S(1)}, u32[]{:S(2)}, u32[]{:S(2)}) collective-permute-start(f32[6,16,8,1]{3,2,1,0:T(8,128)S(1)} %get-tuple-element.85), channel_id=1, source_target_pairs={{8,0},{16,8},{24,16},{32,24},{40,32},{48,40},{56,48},{64,56},{72,6... | collective-permute-start | bytes 9224 | tf_op jit(solution)/shard_map/ppermute | solution.py:27
  16.7 1.9 %collective-permute-start.1 = (f32[6,16,8,1]{3,2,1,0:T(8,128)S(1)}, f32[6,16,8,1]{3,2,1,0:T(8,128)S(1)}, u32[]{:S(2)}, u32[]{:S(2)}) collective-permute-start(f32[6,16,8,1]{3,2,1,0:T(8,128)S(1)} %get-tuple-element.84), channel_id=1, source_target_pairs={{0,8},{8,16},{16,24},{24,32},{32,40},{40,48},{48,56},{56,64},{64,7... | collective-permute-start | bytes 9224 | tf_op jit(solution)/shard_map/ppermute | solution.py:26
  18.7 5.8 %collective-permute-done.2 = f32[6,16,8,1]{3,2,1,0:T(8,128)S(1)} collective-permute-done((f32[6,16,8,1]{3,2,1,0:T(8,128)S(1)}, f32[6,16,8,1]{3,2,1,0:T(8,128)S(1)}, u32[]{:S(2)}, u32[]{:S(2)}) %collective-permute-start.2) | collective-permute-done | bytes 3104 | tf_op jit(solution)/shard_map/ppermute | solution.py:27
  24.5 3.9 %collective-permute-done.1 = f32[6,16,8,1]{3,2,1,0:T(8,128)S(1)} collective-permute-done((f32[6,16,8,1]{3,2,1,0:T(8,128)S(1)}, f32[6,16,8,1]{3,2,1,0:T(8,128)S(1)}, u32[]{:S(2)}, u32[]{:S(2)}) %collective-permute-start.1) | collective-permute-done | bytes 3104 | tf_op jit(solution)/shard_map/ppermute | solution.py:26
  28.5 1.1 %fusion.9 = f32[6,16,10,130]{3,2,1,0:T(8,128)S(1)} fusion(f32[6,16,1,128]{3,2,1,0:T(1,128)S(1)} %collective-permute-done.3, f32[6,16,1,128]{3,2,1,0:T(1,128)S(1)} %collective-permute-done, f32[6,16,8,1]{3,2,1,0:T(8,128)S(1)} %collective-permute-done.2, f32[1,16,8,128]{3,2,1,0:T(8,128)S(1)} %fusion.78, f32[5,16,8,128]{3,2,1,0:T(8,128)S(1)} %slice_bitcast_fusion, ...), kind=kLoop, calls=%fused_computation.15 | loop fusion | flops 1248000 | bytes 996874 | tf_op jit(solution)/shard_map/jit(_where)/select_n | solution.py:85
  30.2 0.7 fusion.147
  32.1 31.5 %all-gather = f32[12,16,8,128]{3,2,1,0:T(8,128)S(1)} all-gather(f32[4,16,8,128]{3,2,1,0:T(8,128)S(1)} %pad_maximum_fusion.5), channel_id=2, replica_groups=mesh['sect'=3,'lon'=32,'lat'=8] {'sect'}, dimensions={0}, use_global_device_ids=true | all-gather | bytes 1048576 | tf_op jit(solution)/shard_map/all_gather | solution.py:39
  64.0 9.0 %collective-permute-start.5 = (f32[8,16,8,2]{3,2,1,0:T(8,128)S(1)}, f32[8,16,8,2]{3,2,1,0:T(8,128)S(1)}, u32[]{:S(2)}, u32[]{:S(2)}) collective-permute-start(f32[8,16,8,2]{3,2,1,0:T(8,128)S(1)} %get-tuple-element.83), channel_id=1, source_target_pairs={{8,0},{16,8},{24,16},{32,24},{40,32},{48,40},{56,48},{64,56},{72,6... | collective-permute-start | bytes 24584 | tf_op jit(solution)/shard_map/ppermute | solution.py:51
  73.0 1.9 %collective-permute-start.4 = (f32[8,16,8,2]{3,2,1,0:T(8,128)S(1)}, f32[8,16,8,2]{3,2,1,0:T(8,128)S(1)}, u32[]{:S(2)}, u32[]{:S(2)}) collective-permute-start(f32[8,16,8,2]{3,2,1,0:T(8,128)S(1)} %get-tuple-element.82), channel_id=1, source_target_pairs={{0,8},{8,16},{16,24},{24,32},{32,40},{40,48},{48,56},{56,64},{64,7... | collective-permute-start | bytes 24584 | tf_op jit(solution)/shard_map/ppermute | solution.py:49
  75.3 4.7 %collective-permute-done.5 = f32[8,16,8,2]{3,2,1,0:T(8,128)S(1)} collective-permute-done((f32[8,16,8,2]{3,2,1,0:T(8,128)S(1)}, f32[8,16,8,2]{3,2,1,0:T(8,128)S(1)}, u32[]{:S(2)}, u32[]{:S(2)}) %collective-permute-start.5) | collective-permute-done | bytes 8224 | tf_op jit(solution)/shard_map/ppermute | solution.py:51
  80.0 6.9 %collective-permute-done.4 = f32[8,16,8,2]{3,2,1,0:T(8,128)S(1)} collective-permute-done((f32[8,16,8,2]{3,2,1,0:T(8,128)S(1)}, f32[8,16,8,2]{3,2,1,0:T(8,128)S(1)}, u32[]{:S(2)}, u32[]{:S(2)}) %collective-permute-start.4) | collective-permute-done | bytes 8224 | tf_op jit(solution)/shard_map/ppermute | solution.py:49
  86.9 0.9 pad_maximum_fusion.4
  87.8 5.0 %collective-permute-start.7 = (f32[8,16,2,132]{3,2,1,0:T(2,128)S(1)}, f32[8,16,2,132]{3,2,1,0:T(2,128)S(1)}, u32[]{:S(2)}, u32[]{:S(2)}) collective-permute-start(f32[8,16,2,132]{3,2,1,0:T(2,128)S(1)} %get-tuple-element.73), channel_id=1, source_target_pairs={{1,0},{2,1},{3,2},{4,3},{5,4},{6,5},{7,6},{0,7},{9,8},{10,9},{11,1... | collective-permute-start | bytes 405512 | tf_op jit(solution)/shard_map/ppermute | solution.py:51
  92.8 1.9 %collective-permute-start.6 = (f32[8,16,2,132]{3,2,1,0:T(2,128)S(1)}, f32[8,16,2,132]{3,2,1,0:T(2,128)S(1)}, u32[]{:S(2)}, u32[]{:S(2)}) collective-permute-start(f32[8,16,2,132]{3,2,1,0:T(2,128)S(1)} %get-tuple-element.72), channel_id=1, source_target_pairs={{0,1},{1,2},{2,3},{3,4},{4,5},{5,6},{6,7},{7,0},{8,9},{9,10},{10,1... | collective-permute-start | bytes 405512 | tf_op jit(solution)/shard_map/ppermute | solution.py:49
  94.7 1.9 %collective-permute-done.7 = f32[8,16,2,132]{3,2,1,0:T(2,128)S(1)} collective-permute-done((f32[8,16,2,132]{3,2,1,0:T(2,128)S(1)}, f32[8,16,2,132]{3,2,1,0:T(2,128)S(1)}, u32[]{:S(2)}, u32[]{:S(2)}) %collective-permute-start.7) | collective-permute-done | bytes 135200 | tf_op jit(solution)/shard_map/ppermute | solution.py:51
  96.7 5.6 %collective-permute-done.6 = f32[8,16,2,132]{3,2,1,0:T(2,128)S(1)} collective-permute-done((f32[8,16,2,132]{3,2,1,0:T(2,128)S(1)}, f32[8,16,2,132]{3,2,1,0:T(2,128)S(1)}, u32[]{:S(2)}, u32[]{:S(2)}) %collective-permute-start.6) | collective-permute-done | bytes 135200 | tf_op jit(solution)/shard_map/ppermute | solution.py:49
  102.3 1.1 %maximum_select_fusion = f32[8,16,12,132]{3,2,1,0:T(8,128)S(1)} fusion(f32[8,16,2,132]{3,2,1,0:T(2,128)S(1)} %collective-permute-done.7, f32[8,16,8,2]{3,2,1,0:T(8,128)S(1)} %collective-permute-done.5, f32[2,16,8,128]{3,2,1,0:T(8,128)S(1)} %slice_bitcast_fusion.9, f32[6,16,8,128]{3,2,1,0:T(8,128)S(1)} %bitcast.204, ...), kind=kLoop, calls=%fused_computation | loop fusion | flops 1216512 | bytes 1622028 | tf_op jit(solution)/shard_map/jit(_where)/select_n | solution.py:85
  104.0 1.7 %fusion.4 = f32[6,16,10,130]{3,2,1,0:T(8,128)S(1)} fusion(f32[8,16,12,132]{3,2,1,0:T(8,128)S(1)} %maximum_select_fusion, f32[16,10,130]{2,1,0:T(8,128)S(1)} %get-tuple-element.102, f32[16,10,130]{2,1,0:T(8,128)S(1)} %get-tuple-element.103, f32[16,10,130]{2,1,0:T(8,128)S(1)} %get-tuple-element.101, f32[16,10,130]{2,1,0:T(8,128)S(1)} %get-tuple-element.100, ...), kind=kLoop, calls=%fused_computation.6 | loop fusion | flops 2121600 | bytes 3660800 | tf_op jit(solution)/shard_map/sub | solution.py:163
  106.8 0.5 multiply_subtract_fusion
  107.5 0.8 multiply_select_fusion
  (65 shorter events, 4.4 us)
Async XLA Ops:
  0.0 18.6 %copy-start.1 = (s32[8,128]{1,0:T(8,128)S(1)}, s32[8,128]{1,0:T(8,128)}, u32[]{:S(2)}) copy-start(s32[8,128]{1,0:T(8,128)} %param.3) | copy-start | bytes 12292
  1.8 26.6 %collective-permute-start.3 = (f32[6,16,1,128]{3,2,1,0:T(1,128)S(1)}, f32[6,16,1,128]{3,2,1,0:T(1,128)S(1)}, u32[]{:S(2)}, u32[]{:S(2)}) collective-permute-start(f32[6,16,1,128]{3,2,1,0:T(1,128)S(1)} %get-tuple-element.87), channel_id=1, source_target_pairs={{1,0},{2,1},{3,2},{4,3},{5,4},{6,5},{7,6},{0,7},{9,8},{10,9},{11,1... | collective-permute-start | bytes 147464 | tf_op jit(solution)/shard_map/ppermute | solution.py:27
  7.2 21.2 %collective-permute-start = (f32[6,16,1,128]{3,2,1,0:T(1,128)S(1)}, f32[6,16,1,128]{3,2,1,0:T(1,128)S(1)}, u32[]{:S(2)}, u32[]{:S(2)}) collective-permute-start(f32[6,16,1,128]{3,2,1,0:T(1,128)S(1)} %get-tuple-element.86), channel_id=1, source_target_pairs={{0,1},{1,2},{2,3},{3,4},{4,5},{5,6},{6,7},{7,0},{8,9},{9,10},{10,1... | collective-permute-start | bytes 147464 | tf_op jit(solution)/shard_map/ppermute | solution.py:26
  9.3 15.2 %collective-permute-start.2 = (f32[6,16,8,1]{3,2,1,0:T(8,128)S(1)}, f32[6,16,8,1]{3,2,1,0:T(8,128)S(1)}, u32[]{:S(2)}, u32[]{:S(2)}) collective-permute-start(f32[6,16,8,1]{3,2,1,0:T(8,128)S(1)} %get-tuple-element.85), channel_id=1, source_target_pairs={{8,0},{16,8},{24,16},{32,24},{40,32},{48,40},{56,48},{64,56},{72,6... | collective-permute-start | bytes 9224 | tf_op jit(solution)/shard_map/ppermute | solution.py:27
  16.7 11.8 %collective-permute-start.1 = (f32[6,16,8,1]{3,2,1,0:T(8,128)S(1)}, f32[6,16,8,1]{3,2,1,0:T(8,128)S(1)}, u32[]{:S(2)}, u32[]{:S(2)}) collective-permute-start(f32[6,16,8,1]{3,2,1,0:T(8,128)S(1)} %get-tuple-element.84), channel_id=1, source_target_pairs={{0,8},{8,16},{16,24},{24,32},{32,40},{40,48},{48,56},{56,64},{64,7... | collective-permute-start | bytes 9224 | tf_op jit(solution)/shard_map/ppermute | solution.py:26
  31.0 1.0 copy-start
  64.0 16.1 %collective-permute-start.5 = (f32[8,16,8,2]{3,2,1,0:T(8,128)S(1)}, f32[8,16,8,2]{3,2,1,0:T(8,128)S(1)}, u32[]{:S(2)}, u32[]{:S(2)}) collective-permute-start(f32[8,16,8,2]{3,2,1,0:T(8,128)S(1)} %get-tuple-element.83), channel_id=1, source_target_pairs={{8,0},{16,8},{24,16},{32,24},{40,32},{48,40},{56,48},{64,56},{72,6... | collective-permute-start | bytes 24584 | tf_op jit(solution)/shard_map/ppermute | solution.py:51
  73.0 13.9 %collective-permute-start.4 = (f32[8,16,8,2]{3,2,1,0:T(8,128)S(1)}, f32[8,16,8,2]{3,2,1,0:T(8,128)S(1)}, u32[]{:S(2)}, u32[]{:S(2)}) collective-permute-start(f32[8,16,8,2]{3,2,1,0:T(8,128)S(1)} %get-tuple-element.82), channel_id=1, source_target_pairs={{0,8},{8,16},{16,24},{24,32},{32,40},{40,48},{48,56},{56,64},{64,7... | collective-permute-start | bytes 24584 | tf_op jit(solution)/shard_map/ppermute | solution.py:49
  87.8 8.9 %collective-permute-start.7 = (f32[8,16,2,132]{3,2,1,0:T(2,128)S(1)}, f32[8,16,2,132]{3,2,1,0:T(2,128)S(1)}, u32[]{:S(2)}, u32[]{:S(2)}) collective-permute-start(f32[8,16,2,132]{3,2,1,0:T(2,128)S(1)} %get-tuple-element.73), channel_id=1, source_target_pairs={{1,0},{2,1},{3,2},{4,3},{5,4},{6,5},{7,6},{0,7},{9,8},{10,9},{11,1... | collective-permute-start | bytes 405512 | tf_op jit(solution)/shard_map/ppermute | solution.py:51
  92.8 9.5 %collective-permute-start.6 = (f32[8,16,2,132]{3,2,1,0:T(2,128)S(1)}, f32[8,16,2,132]{3,2,1,0:T(2,128)S(1)}, u32[]{:S(2)}, u32[]{:S(2)}) collective-permute-start(f32[8,16,2,132]{3,2,1,0:T(2,128)S(1)} %get-tuple-element.72), channel_id=1, source_target_pairs={{0,1},{1,2},{2,3},{3,4},{4,5},{5,6},{6,7},{7,0},{8,9},{9,10},{10,1... | collective-permute-start | bytes 405512 | tf_op jit(solution)/shard_map/ppermute | solution.py:49
where the time goes:
time: 109 us; the launch traced here: 108 us
  starting transfers between devices  34.3 us (31%)
  blocking collectives  31.5 us (29%)
  waiting for transfers between devices  28.9 us (27%)
  other arithmetic  11.1 us (10%)
  local copies, waits for them, and re-layouts  1.85 us (2%)
    all_gather x1, blocking collectives, picked(): lax.all_gather(shard, axis)  31.5 us
    ppermute x2, starting transfers between devices, with_halo(): lax.ppermute(head, axis, [((i + 1) % count, i) for i in range(count)])  14 us
    ppermute x2, starting transfers between devices, padded(): lax.ppermute(initial, axis, [(b, a) for a, b in up])  12.7 us
    ppermute x2, waiting for transfers between devices, with_halo(): lax.ppermute(tail, axis, [(i, (i + 1) % count) for i in range(count)])  12.5 us
    ppermute x2, waiting for transfers between devices, with_halo(): lax.ppermute(head, axis, [((i + 1) % count, i) for i in range(count)])  6.66 us
    ppermute x2, waiting for transfers between devices, padded(): lax.ppermute(initial, axis, [(b, a) for a, b in up])  5.84 us
    ppermute x2, waiting for transfers between devices, padded(): lax.ppermute(last, axis, up)  3.95 us
    ppermute x2, starting transfers between devices, padded(): lax.ppermute(last, axis, up)  3.84 us
  transfers between devices with their start and end apart: 8, of which 6 were waited for; matrix products, arithmetic and copies ran while one was open for 1% of the time, Pallas kernels for 0%

commit v1 on v0

v1 whole, which is shorter than its diff:
```python
import functools

import jax
import jax.numpy as jnp
from jax import lax
from jax.experimental import pallas as pl
from jax.experimental.pallas import tpu as pltpu
from jax.sharding import PartitionSpec as P

MESH = pl.DeviceIdType.MESH
F32 = jnp.float32
K = 16
NF = 6
NT = NF * K
SUB = 0.5
N_ROW = NT + 8

(R_COL_W, R_COL_E, R_NEAR_S, R_NEAR_N, R_FAR_S, R_FAR_N, R_CORNER_S, R_CORNER_N) = range(8)
N_HALO = 8
(Z_ZON, Z_MER, Z_ROW_S, Z_FAR_S, Z_ROW_N, Z_COL, Z_DIFF) = range(7)
N_Z = 7


def tile(t):
    return pl.ds(pl.multiple_of(t * 8, 8), 8)


def lroll(x, amount):
    return pltpu.roll(x, amount, 1)


def sroll(x, amount):
    return pltpu.roll(x, amount, 0)


def face(level, limit, speed):
    return jnp.where(level < limit, speed, 0.0)


def coefficients(fe, fw, fn, fs):
    ce = -SUB * jnp.minimum(fe, 0.0)
    cw = SUB * jnp.maximum(fw, 0.0)
    cn = -SUB * jnp.minimum(fn, 0.0)
    cs = SUB * jnp.maximum(fs, 0.0)
    out = (jnp.maximum(fe, 0.0) - jnp.minimum(fw, 0.0)) + (jnp.maximum(fn, 0.0) - jnp.minimum(fs, 0.0))
    return 1.0 - SUB * out, ce, cw, cn, cs


def combine(c, q, qe, qw, qn, qs):
    c0, ce, cw, cn, cs = c
    return (c0 * q + (ce * qe + cw * qw)) + (cn * qn + cs * qs)


def kernel(n_sect, n_lon, n_lat, x_hbm, lev_ref, out,
           x, cols, cols_w, cols_e, rows_out, rows, near, far, corner_s, corner_n,
           zm, flow_rows, flow_cols, flow_cols_out, diff, rhs, div, ratio, ring_cols, ring_rows,
           in_sem, send_sem, recv_sem, zsend_sem, zrecv_sem):
    sect = lax.axis_index("sect")
    lon = lax.axis_index("lon")
    lat = lax.axis_index("lat")
    east = lax.rem(lon + 1, n_lon)
    west = lax.rem(lon + n_lon - 1, n_lon)
    has_s = lat > 0
    has_n = lat < n_lat - 1

    barrier = pltpu.get_barrier_semaphore()
    for step in range(1, n_sect):
        pl.semaphore_signal(barrier, inc=1, device_id={"sect": lax.rem(sect + step, n_sect)}, device_id_type=MESH)
    for side in (east, west):
        pl.semaphore_signal(barrier, inc=1, device_id={"lon": side}, device_id_type=MESH)

    @pl.when(has_s)
    def _():
        pl.semaphore_signal(barrier, inc=1, device_id={"lat": lat - 1}, device_id_type=MESH)

    @pl.when(has_n)
    def _():
        pl.semaphore_signal(barrier, inc=1, device_id={"lat": lat + 1}, device_id_type=MESH)

    load = pltpu.make_async_copy(x_hbm, x, in_sem)
    load.start()

    lane = lax.broadcasted_iota(jnp.int32, (8, 128), 1)
    row = lax.broadcasted_iota(jnp.int32, (8, 128), 0)
    even = (lane & 1) == 0
    pair = 63 - (lane >> 1)
    pair_b = 63 - (jnp.where(even, (lane + 126) >> 1, (lane + 1) >> 1) & 63)
    first_lane, last_lane = lane == 0, lane == 127
    first_row, last_row = row == 0, row == 7
    lev = lev_ref[...].astype(F32)
    zero = jnp.zeros((8, 128), F32)

    def bcast(value):
        return jnp.broadcast_to(value, (8, 128))

    @pl.when(jnp.logical_not(has_s))
    def _():
        rows[0] = jnp.zeros((N_ROW, 128), F32)
        rows[2] = jnp.zeros((N_ROW, 128), F32)
        corner_s[...] = jnp.zeros((16, 128), F32)

    @pl.when(jnp.logical_not(has_n))
    def _():
        rows[1] = jnp.zeros((N_ROW, 128), F32)
        rows[3] = jnp.zeros((N_ROW, 128), F32)
        corner_n[...] = jnp.zeros((16, 128), F32)

    load.wait()

    def pack(acc, value, turn, p):
        a, b = acc
        turned = lroll(value, turn)
        return jnp.where(pair == p, turned, a), jnp.where(pair_b == p, turned, b)

    def pack_level(k, carry):
        a0, a1, b0, b1 = carry
        for f in range(NF):
            p = (f % 4) * K + k
            value = x[tile(f * K + k), :]
            if f < 4:
                a0, b0 = pack((a0, b0), value, 127 - 2 * p, p)
            else:
                a1, b1 = pack((a1, b1), value, 127 - 2 * p, p)
        return a0, a1, b0, b1

    a0, a1, b0, b1 = lax.fori_loop(0, K, pack_level, (zero,) * 4)
    a1, b1 = pack((a1, b1), lev, 63, 32)
    for i, value in enumerate((a0, a1, b0, b1)):
        cols[i * 8:i * 8 + 8, :] = value

    def pack_rows(u, carry):
        for i, r in enumerate((7, 0, 6, 1)):
            rows_out[i, tile(u), :] = x[pl.ds(u * 64 + r, 8, stride=8), :]
        return carry

    lax.fori_loop(0, NT // 8, pack_rows, 0)
    for i, r in enumerate((7, 0, 6, 1)):
        rows_out[i, NT:NT + 8, :] = bcast(lev[r:r + 1, :])

    pl.semaphore_wait(barrier, n_sect + 1 + has_s.astype(jnp.int32) + has_n.astype(jnp.int32))

    def remote(src, dst, send, recv, to):
        return pltpu.make_async_remote_copy(src_ref=src, dst_ref=dst, send_sem=send, recv_sem=recv, device_id=to,
                                            device_id_type=MESH)

    def halo(src, dst, slot, to):
        return remote(src, dst, send_sem.at[slot], recv_sem.at[slot], to)

    south, north = {"lat": lat - 1}, {"lat": lat + 1}
    from_w = halo(cols, cols_w, R_COL_W, {"lon": east})
    from_e = halo(cols, cols_e, R_COL_E, {"lon": west})
    near_s = halo(rows_out.at[0], rows.at[0], R_NEAR_S, north)
    near_n = halo(rows_out.at[1], rows.at[1], R_NEAR_N, south)
    far_s = halo(rows_out.at[2], rows.at[2], R_FAR_S, north)
    far_n = halo(rows_out.at[3], rows.at[3], R_FAR_N, south)
    edge_s = halo(near, corner_s, R_CORNER_S, north)
    edge_n = halo(near, corner_n, R_CORNER_N, south)

    def across(slot, peer):
        to = {"sect": peer}
        src, dst = (
            (x_hbm.at[0:K * 8], zm.at[0:K * 8]),
            (x_hbm.at[K * 8:2 * K * 8], zm.at[K * 8:2 * K * 8]),
            (rows.at[0, 0:2 * K], flow_rows.at[0:2 * K]),
            (rows.at[2, K:2 * K], flow_rows.at[2 * K:3 * K]),
            (rows.at[1, 0:2 * K], flow_rows.at[3 * K:5 * K]),
            (flow_cols_out, flow_cols),
            (diff, diff),
        )[slot]
        return remote(src, dst, zsend_sem.at[peer - 1, slot], zrecv_sem.at[slot], to)

    def to_tracers(*slots):
        for slot in slots:
            for peer in range(1, n_sect):
                across(slot, peer).start()

    from_w.start()
    from_e.start()

    @pl.when(has_n)
    def _():
        near_s.start()

    @pl.when(has_s)
    def _():
        near_n.start()

    @pl.when(sect == 0)
    def _():
        to_tracers(Z_ZON, Z_MER)

    @pl.when(has_n)
    def _():
        far_s.start()

    @pl.when(has_s)
    def _():
        far_n.start()

    from_w.wait_recv()
    from_e.wait_recv()
    for v in range(2):
        a, b = slice(v * 8, v * 8 + 8), slice(16 + v * 8, 24 + v * 8)
        near[a, :] = jnp.where(even, lroll(cols_e[a, :], 127), lroll(cols_w[a, :], 1))
        far[a, :] = jnp.where(even, lroll(cols_e[b, :], 126), lroll(cols_w[b, :], 2))

    @pl.when(has_n)
    def _():
        edge_s.start()

    @pl.when(has_s)
    def _():
        edge_n.start()

    @pl.when(has_s)
    def _():
        near_s.wait_recv()

    @pl.when(has_n)
    def _():
        near_n.wait_recv()

    def neighbours(q, f, k, columns, south_ref, north_ref):
        v = (f // 4) * 8
        p = (f % 4) * K + k
        side = lroll(columns[v:v + 8, :], 2 * p + 1)
        return (
            jnp.where(last_lane, side, lroll(q, 127)),
            jnp.where(first_lane, side, lroll(q, 1)),
            jnp.where(last_row, bcast(north_ref[pl.ds(f * K + k, 1), :]), sroll(q, 7)),
            jnp.where(first_row, bcast(south_ref[pl.ds(f * K + k, 1), :]), sroll(q, 1)),
        )

    side = lroll(near[8:16, :], 65)
    lev_e = jnp.where(last_lane, side, lroll(lev, 127))
    lev_w = jnp.where(first_lane, side, lroll(lev, 1))
    lev_n = jnp.where(last_row, rows[1, NT:NT + 8, :], sroll(lev, 7))
    lev_s = jnp.where(first_row, rows[0, NT:NT + 8, :], sroll(lev, 1))
    lim_e, lim_w = jnp.minimum(lev, lev_e), jnp.minimum(lev, lev_w)
    lim_n, lim_s = jnp.minimum(lev, lev_n), jnp.minimum(lev, lev_s)

    @pl.when(sect == 0)
    def _():
        def around(f, k):
            q = x[tile(f * K + k), :]
            return q, neighbours(q, f, k, near, rows.at[0], rows.at[1])

        def conductances(k, level):
            v, (ve, vw, vn, vs) = around(4, k)
            return (face(level, lim_e, 0.5 * (v + ve)), face(level, lim_w, 0.5 * (vw + v)),
                    face(level, lim_n, 0.5 * (v + vn)), face(level, lim_s, 0.5 * (vs + v)))

        def diffuse(c, q, sides):
            ce, cw, cn, cs = c
            qe, qw, qn, qs = sides
            return ce * (qe - q) - cw * (q - qw) + cn * (qn - q) - cs * (q - qs)

        def warm(k, above):
            level = lax.convert_element_type(k, F32)
            c = conductances(k, level)
            t, sides = around(2, k)
            new = t + diffuse(c, t, sides)
            out[tile(2 * K + k), :] = new
            jump = 0.2 * (above - new)
            wet = jnp.where((level < lev) & (k > 0), x[tile(5 * K + k), :], 0.0)
            mixing = wet * (1.0 + 4.0 / (1.0 + jump * jump))
            out[tile(5 * K + k), :] = mixing
            diff[tile(k), :] = mixing
            return new

        lax.fori_loop(0, K, warm, zero)

        @pl.when(has_s)
        def _():
            far_s.wait_recv()
            edge_s.wait_recv()

        @pl.when(has_n)
        def _():
            far_n.wait_recv()
            edge_n.wait_recv()

        for i, value in enumerate((cols[0:8, :], near[0:8, :], far[0:8, :], corner_s[0:8, :], corner_n[0:8, :])):
            flow_cols_out[i * 8:i * 8 + 8, :] = value
        to_tracers(Z_ROW_S, Z_FAR_S, Z_ROW_N, Z_COL, Z_DIFF)

        def move(k, sums):
            level = lax.convert_element_type(k, F32)
            c = conductances(k, level)
            z, zs = around(0, k)
            m, ms = around(1, k)
            t, ts = around(2, k)
            s, ss = around(3, k)
            out[tile(3 * K + k), :] = s + diffuse(c, s, ss)
            here, at_e, at_n = sums

            def add(total, limit, sal, tem):
                return total + jnp.where(level < limit, 0.15 * sal - 0.2 * tem, 0.0)

            here = add(here, lev, s, t)
            at_e = add(at_e, lev_e, ss[0], ts[0])
            at_n = add(at_n, lev_n, ss[2], ts[2])
            new_z = z + (diffuse(c, z, zs) + 0.3 * m - 0.05 * (at_e - here))
            new_m = m + (diffuse(c, m, ms) - 0.3 * z - 0.05 * (at_n - here))
            out[tile(k), :] = face(level, lim_e, new_z)
            out[tile(K + k), :] = face(level, lim_n, new_m)
            div[tile(k), :] = (face(level, lim_e, z) - face(level, lim_w, zs[1])) + (
                face(level, lim_n, m) - face(level, lim_s, ms[3]))
            return here, at_e, at_n

        lax.fori_loop(0, K, move, (zero,) * 3)

        def rise(i, total):
            k = K - 1 - i
            total = total + div[tile(k), :]
            out[tile(4 * K + k), :] = jnp.where(k > 0, -total, 0.0)
            return total

        lax.fori_loop(0, K, rise, zero)

    @pl.when(sect != 0)
    def _():
        @pl.when(has_s)
        def _():
            far_s.wait_recv()
            edge_s.wait_recv()

        @pl.when(has_n)
        def _():
            far_n.wait_recv()
            edge_n.wait_recv()

        for slot in (Z_ROW_S, Z_FAR_S, Z_ROW_N, Z_COL, Z_ZON, Z_MER):
            across(slot, 1).wait_recv()

        p1_lev = jnp.where(even, bcast(near[8:16, 62:63]), bcast(near[8:16, 63:64]))
        p2_lev = jnp.where(even, bcast(far[8:16, 62:63]), bcast(far[8:16, 63:64]))
        p0_lev = jnp.where(even, bcast(cols[8:16, 62:63]), bcast(cols[8:16, 63:64]))
        cs_lev = jnp.where(even, bcast(corner_s[8:16, 62:63]), bcast(corner_s[8:16, 63:64]))
        cn_lev = jnp.where(even, bcast(corner_n[8:16, 62:63]), bcast(corner_n[8:16, 63:64]))

        def up_one(value, beyond):
            return jnp.where(last_row, sroll(beyond, 7), sroll(value, 7))

        def down_one(value, beyond):
            return jnp.where(first_row, sroll(beyond, 1), sroll(value, 1))

        def repeat(value, offset):
            if offset:
                value = lroll(value, offset)
            value = jnp.where(lane >= 96, value, 0.0)
            value = value + lroll(value, 32)
            return value + lroll(value, 64)

        p0_z, p1_z, p2_z = (repeat(flow_cols[i * 8:i * 8 + 8, :], 0) for i in range(3))
        p1_m, cs_m, cn_m = (repeat(flow_cols[i * 8:i * 8 + 8, :], 32) for i in (1, 3, 4))
        k_lane = (pair & (K - 1)).astype(F32)
        lim = functools.partial(jnp.minimum, p1_lev)
        c = coefficients(
            face(k_lane, lim(jnp.where(even, p2_lev, p0_lev)), p1_z),
            face(k_lane, lim(jnp.where(even, p0_lev, p2_lev)), jnp.where(even, p0_z, p2_z)),
            face(k_lane, lim(up_one(p1_lev, cn_lev)), p1_m),
            face(k_lane, lim(down_one(p1_lev, cs_lev)), down_one(p1_m, cs_m)),
        )
        for v in range(2):
            a = slice(v * 8, v * 8 + 8)
            p0, p1, p2 = cols[a, :], near[a, :], far[a, :]
            ring_cols[a, :] = combine(c, p1, jnp.where(even, p2, p0), jnp.where(even, p0, p2),
                                      up_one(p1, corner_n[a, :]), down_one(p1, corner_s[a, :]))

        def corner_of(value, at, p):
            return pltpu.roll(bcast(value[at:at + 1, :]), 2 * p + 1, 1, stride=2, stride_axis=0)

        def turn(value, corner):
            return jnp.where(last_lane, corner, lroll(value, 127)), jnp.where(first_lane, corner, lroll(value, 1))

        for north_side in range(2):
            at = 0 if north_side else 7
            corner = corner_n if north_side else corner_s
            corner_z = flow_cols[32:40, :] if north_side else flow_cols[24:32, :]
            base = 3 * K if north_side else 0
            r_lev = rows[north_side, NT:NT + 8, :]
            r_in = rows_out[1 - north_side, NT:NT + 8, :]
            r_out = rows[2 + north_side, NT:NT + 8, :]
            r_e, r_w = turn(r_lev, lroll(bcast(corner[8 + at:9 + at, :]), 65))
            for octet in range(2):
                k_row = (row + 8 * octet).astype(F32)
                z = flow_rows[base + octet * 8:base + octet * 8 + 8, :]
                m = flow_rows[base + K + octet * 8:base + K + octet * 8 + 8, :]
                _, zw = turn(z, corner_of(corner_z, at, octet * 8))
                lim_in, lim_out = jnp.minimum(r_lev, r_in), jnp.minimum(r_lev, r_out)
                if north_side:
                    inner = zm[pl.ds(K * 8 + octet * 64 + 7, 8, stride=8), :]
                    fn, fs = face(k_row, lim_out, m), face(k_row, lim_in, inner)
                else:
                    outer = flow_rows[2 * K + octet * 8:2 * K + octet * 8 + 8, :]
                    fn, fs = face(k_row, lim_in, m), face(k_row, lim_out, outer)
                c = coefficients(face(k_row, jnp.minimum(r_lev, r_e), z), face(k_row, jnp.minimum(r_lev, r_w), zw), fn, fs)
                for f in range(NF):
                    v, p, u = f // 4, (f % 4) * K + octet * 8, (f * K + octet * 8)
                    a = slice(u, u + 8)
                    q, inner, outer = rows[north_side, a, :], rows_out[1 - north_side, a, :], rows[2 + north_side, a, :]
                    qe, qw = turn(q, corner_of(corner[v * 8:v * 8 + 8, :], at, p))
                    qn, qs = (outer, inner) if north_side else (inner, outer)
                    ring_rows[north_side, a, :] = combine(c, q, qe, qw, qn, qs)

        def advance(k, carry):
            level = lax.convert_element_type(k, F32)
            z, m = zm[tile(k), :], zm[tile(K + k), :]
            side = lroll(flow_cols[8:16, :], 2 * k + 1)
            zw = jnp.where(first_lane, side, lroll(z, 1))
            ms = jnp.where(first_row, bcast(flow_rows[pl.ds(K + k, 1), :]), sroll(m, 1))
            fe, fw, fn, fs = face(level, lim_e, z), face(level, lim_w, zw), face(level, lim_n, m), face(level, lim_s, ms)
            div[tile(k), :] = (fe - fw) + (fn - fs)
            c = coefficients(fe, fw, fn, fs)
            for f in range(NF):
                q = x[tile(f * K + k), :]
                q = combine(c, q, *neighbours(q, f, k, near, rows.at[0], rows.at[1]))
                q = combine(c, q, *neighbours(q, f, k, ring_cols, ring_rows.at[0], ring_rows.at[1]))
                rhs[tile(f * K + k), :] = q
            return carry

        lax.fori_loop(0, K, advance, 0)
        across(Z_DIFF, 1).wait_recv()

        def eliminate(i, carry):
            total, up_below, down_below, ratio_below, below = carry
            k = K - 1 - i
            total = total + div[tile(k), :]
            kappa = diff[tile(k), :]
            vertical = jnp.where(k > 0, -total, 0.0)
            up = jnp.maximum(vertical, 0.0) + kappa
            down = jnp.minimum(vertical, 0.0) - kappa
            inverse = 1.0 / ((1.0 + (up - down_below)) + up_below * ratio_below)
            here = down * inverse
            ratio[tile(k), :] = here
            values = []
            for f in range(NF):
                value = (rhs[tile(f * K + k), :] + up_below * below[f]) * inverse
                rhs[tile(f * K + k), :] = value
                values.append(value)
            return total, up, down, here, tuple(values)

        lax.fori_loop(0, K, eliminate, (zero,) * 4 + ((zero,) * NF,))

        def settle(k, above):
            level = lax.convert_element_type(k, F32)
            here = ratio[tile(k), :]
            values = []
            for f in range(NF):
                value = rhs[tile(f * K + k), :] - here * above[f]
                out[tile(f * K + k), :] = face(level, lev, value)
                values.append(value)
            return tuple(values)

        lax.fori_loop(0, K, settle, (zero,) * NF)

    from_w.wait_send()
    from_e.wait_send()

    @pl.when(has_n)
    def _():
        for copy in (near_s, far_s, edge_s):
            copy.wait_send()

    @pl.when(has_s)
    def _():
        for copy in (near_n, far_n, edge_n):
            copy.wait_send()

    @pl.when(sect == 0)
    def _():
        for slot in range(N_Z):
            for peer in range(1, n_sect):
                across(slot, peer).wait_send()


def solution(mesh):
    n_sect, n_lon, n_lat = (mesh.shape[a] for a in ("sect", "lon", "lat"))

    def on_device(fields, levels):
        vmem = pltpu.VMEM
        result = pl.pallas_call(
            functools.partial(kernel, n_sect, n_lon, n_lat),
            out_shape=jax.ShapeDtypeStruct((NT * 8, 128), F32),
            in_specs=[pl.BlockSpec(memory_space=pl.ANY), pl.BlockSpec(memory_space=pltpu.VMEM)],
            out_specs=pl.BlockSpec(memory_space=pltpu.VMEM),
            scratch_shapes=[
                vmem((NT * 8, 128), F32),
                vmem((32, 128), F32),
                vmem((32, 128), F32),
                vmem((32, 128), F32),
                vmem((4, N_ROW, 128), F32),
                vmem((4, N_ROW, 128), F32),
                vmem((16, 128), F32),
                vmem((16, 128), F32),
                vmem((16, 128), F32),
                vmem((16, 128), F32),
                vmem((2 * K * 8, 128), F32),
                vmem((5 * K, 128), F32),
                vmem((40, 128), F32),
                vmem((40, 128), F32),
                vmem((K * 8, 128), F32),
                vmem((NT * 8, 128), F32),
                vmem((K * 8, 128), F32),
                vmem((K * 8, 128), F32),
                vmem((16, 128), F32),
                vmem((2, NT, 128), F32),
                pltpu.SemaphoreType.DMA,
                pltpu.SemaphoreType.DMA((N_HALO,)),
                pltpu.SemaphoreType.DMA((N_HALO,)),
                pltpu.SemaphoreType.DMA((n_sect - 1, N_Z)),
                pltpu.SemaphoreType.DMA((N_Z,)),
            ],
            compiler_params=pltpu.CompilerParams(collective_id=0, has_side_effects=True),
        )(fields.reshape(NT * 8, 128), levels)
        return result.reshape(1, NF, K, 8, 128)

    return jax.shard_map(
        on_device,
        mesh=mesh,
        in_specs=(P("sect", None, None, "lat", "lon"), P("lat", "lon")),
        out_specs=P("sect", None, None, "lat", "lon"),
        check_vma=False,
    )
```

time: 109 us -> 39.5 us (0.36)
  the two profiles are of different devices: /device:TPU:6 before, /device:TPU:1 now
where the time goes in v1:
time: 39.5 us; the launch traced here: 39.3 us
  Pallas kernels  37.5 us (95%)
  local copies, waits for them, and re-layouts  1.77 us (4%)
    pallas_call x1, Pallas kernels, on_device(): pl.pallas_call(functools.partial(kernel, n_sect, n_lon, n_lat), out_shape...  37.5 us
    unnamed x1, local copies, waits for them, and re-layouts  1.77 us

profile of v1, /device:TPU:1, one launch (start us, length us, event | category | flops | bytes accessed | tf_op | source)
XLA Modules:
  0.0 39.3 jit_solution(12008044472923970336)
XLA Ops:
  0.0 37.5 %shard_map.28 = f32[768,128]{1,0:T(8,128)} custom-call(f32[768,128]{1,0:T(8,128)} %bitcast.3, s32[8,128]{1,0:T(8,128)} %lev_ref.1), custom_call_target="tpu_custom_call" | custom-call | tf_op jit(solution)/shard_map/pallas_call | solution.py:483
  37.5 1.8 %copy.4 = f32[1,6,16,8,128]{4,3,2,1,0:T(8,128)} copy(f32[1,6,16,8,128]{4,3,2,1,0:T(8,128)} %bitcast.2) | data formatting | bytes 786432

commit v2 on v1

--- a/solution.py
+++ b/solution.py
@@ -15,10 +15,13 @@
 SUB = 0.5
 N_ROW = NT + 8
 
-(R_COL_W, R_COL_E, R_NEAR_S, R_NEAR_N, R_FAR_S, R_FAR_N, R_CORNER_S, R_CORNER_N) = range(8)
-N_HALO = 8
-(Z_ZON, Z_MER, Z_ROW_S, Z_FAR_S, Z_ROW_N, Z_COL, Z_DIFF) = range(7)
-N_Z = 7
+(R_COL_W, R_COL_E, R_NEAR_S, R_NEAR_N, R_FAR_S, R_FAR_N, R_CORNER_S, R_CORNER_N, R_FLOW_S, R_FLOW_N) = (*range(8), 8, 10)
+N_HALO = 12
+CH = 2
+NC = K // CH
+DV = 3
+Z_PART, Z_COL, Z_DIFF = 2 * NC, 2 * NC + 2, 2 * NC + 3
+N_Z = 2 * NC + 4
 
 
 def tile(t):
@@ -53,8 +56,8 @@
 
 def kernel(n_sect, n_lon, n_lat, x_hbm, lev_ref, out,
            x, cols, cols_w, cols_e, rows_out, rows, near, far, corner_s, corner_n,
-           zm, flow_rows, flow_cols, flow_cols_out, diff, rhs, div, ratio, ring_cols, ring_rows,
-           in_sem, send_sem, recv_sem, zsend_sem, zrecv_sem):
+           zm, flow_rows, flow_rows_out, flow_cols, flow_cols_out, diff, rhs, div, ratio, ring_cols, ring_rows,
+           in_sem, send_sem, recv_sem, zsend_sem, zsend2_sem, zrecv_sem):
     sect = lax.axis_index("sect")
     lon = lax.axis_index("lon")
     lat = lax.axis_index("lat")
@@ -98,12 +101,14 @@
         rows[0] = jnp.zeros((N_ROW, 128), F32)
         rows[2] = jnp.zeros((N_ROW, 128), F32)
         corner_s[...] = jnp.zeros((16, 128), F32)
+        flow_rows[:, 0:24, :] = jnp.zeros((2, 24, 128), F32)
 
     @pl.when(jnp.logical_not(has_n))
     def _():
         rows[1] = jnp.zeros((N_ROW, 128), F32)
         rows[3] = jnp.zeros((N_ROW, 128), F32)
         corner_n[...] = jnp.zeros((16, 128), F32)
+        flow_rows[:, 24:40, :] = jnp.zeros((2, 16, 128), F32)
 
     load.wait()
 
@@ -156,23 +161,36 @@
     edge_s = halo(near, corner_s, R_CORNER_S, north)
     edge_n = halo(near, corner_n, R_CORNER_N, south)
 
-    def across(slot, peer):
-        to = {"sect": peer}
-        src, dst = (
-            (x_hbm.at[0:K * 8], zm.at[0:K * 8]),
-            (x_hbm.at[K * 8:2 * K * 8], zm.at[K * 8:2 * K * 8]),
-            (rows.at[0, 0:2 * K], flow_rows.at[0:2 * K]),
-            (rows.at[2, K:2 * K], flow_rows.at[2 * K:3 * K]),
-            (rows.at[1, 0:2 * K], flow_rows.at[3 * K:5 * K]),
-            (flow_cols_out, flow_cols),
-            (diff, diff),
-        )[slot]
-        return remote(src, dst, zsend_sem.at[peer - 1, slot], zrecv_sem.at[slot], to)
-
-    def to_tracers(*slots):
-        for slot in slots:
-            for peer in range(1, n_sect):
-                across(slot, peer).start()
+    def flow_s(octet):
+        return halo(flow_rows_out.at[octet, 0:24], flow_rows.at[octet, 0:24], R_FLOW_S + octet, north)
+
+    def flow_n(octet):
+        return halo(flow_rows_out.at[octet, 24:40], flow_rows.at[octet, 24:40], R_FLOW_N + octet, south)
+
+    def across(src, dst, slot, peer):
+        return remote(src, dst, zsend_sem.at[slot], zrecv_sem.at[slot], {"sect": peer})
+
+    def rows_of(ref, start, size):
+        return ref.at[pl.ds(pl.multiple_of(start * 8, 8), size * 8)]
+
+    def speed(field, c):
+        return across(rows_of(x_hbm, field * K + c * CH, CH), rows_of(zm, field * K + c * CH, CH), field * NC + c, field + 1)
+
+    def speed_on(field, c, peer):
+        part = rows_of(zm, field * K + c * CH, CH)
+        return across(part, part, field * NC + c, peer)
+
+    def part_of(field, peer):
+        part = rows_of(diff, field * DV, DV)
+        return across(part, part, Z_PART + field, peer)
+
+    def both(slot, src, dst):
+        return [remote(src, dst, zsend2_sem.at[peer - 1, slot - Z_COL], zrecv_sem.at[slot], {"sect": peer})
+                for peer in range(1, n_sect)]
+
+    send_cols = both(Z_COL, flow_cols_out, flow_cols)
+    rest = slice(2 * DV * 8, K * 8)
+    send_diff = both(Z_DIFF, diff.at[rest], diff.at[rest])
 
     from_w.start()
     from_e.start()
@@ -187,13 +205,15 @@
 
     @pl.when(sect == 0)
     def _():
-        to_tracers(Z_ZON, Z_MER)
-
-    @pl.when(has_n)
+        for c in range(NC):
+            for field in range(2):
+                speed(field, c).start()
+
+    @pl.when(has_n & (sect != 0))
     def _():
         far_s.start()
 
-    @pl.when(has_s)
+    @pl.when(has_s & (sect != 0))
     def _():
         far_n.start()
 
@@ -270,19 +290,22 @@
 
         lax.fori_loop(0, K, warm, zero)
 
+        for field in range(2):
+            part_of(field, field + 1).start()
+
         @pl.when(has_s)
         def _():
-            far_s.wait_recv()
             edge_s.wait_recv()
 
         @pl.when(has_n)
         def _():
-            far_n.wait_recv()
             edge_n.wait_recv()
 
-        for i, value in enumerate((cols[0:8, :], near[0:8, :], far[0:8, :], corner_s[0:8, :], corner_n[0:8, :])):
-            flow_cols_out[i * 8:i * 8 + 8, :] = value
-        to_tracers(Z_ROW_S, Z_FAR_S, Z_ROW_N, Z_COL, Z_DIFF)
+        flow_cols_out[0:8, :] = jnp.where(
+            lane >= 64, near[0:8, :], jnp.where(lane >= 32, lroll(far[0:8, :], 64), lroll(cols[0:8, :], 32)))
+        flow_cols_out[8:16, :] = jnp.where(first_row, corner_n[0:8, :], corner_s[0:8, :])
+        for copy in send_cols + send_diff:
+            copy.start()
 
         def move(k, sums):
             level = lax.convert_element_type(k, F32)
@@ -320,6 +343,13 @@
 
     @pl.when(sect != 0)
     def _():
+        own, peer = sect - 1, 3 - sect
+        for c in range(NC):
+            speed_on(own, c, peer).wait_recv()
+            speed_on(own, c, peer).start()
+        part_of(own, peer).wait_recv()
+        part_of(own, peer).start()
+
         @pl.when(has_s)
         def _():
             far_s.wait_recv()
@@ -330,8 +360,22 @@
             far_n.wait_recv()
             edge_n.wait_recv()
 
-        for slot in (Z_ROW_S, Z_FAR_S, Z_ROW_N, Z_COL, Z_ZON, Z_MER):
-            across(slot, 1).wait_recv()
+        def share_rows(octet):
+            for c in range(octet * NC // 2, (octet + 1) * NC // 2):
+                speed_on(1 - own, c, peer).wait_recv()
+            for i, (field, r) in enumerate(((0, 7), (1, 7), (1, 6), (0, 0), (1, 0))):
+                flow_rows_out[octet, i * 8:i * 8 + 8, :] = zm[pl.ds((field * K + octet * 8) * 8 + r, 8, stride=8), :]
+
+            @pl.when(has_n)
+            def _():
+                flow_s(octet).start()
+
+            @pl.when(has_s)
+            def _():
+                flow_n(octet).start()
+
+        share_rows(0)
+        send_cols[0].wait_recv()
 
         p1_lev = jnp.where(even, bcast(near[8:16, 62:63]), bcast(near[8:16, 63:64]))
         p2_lev = jnp.where(even, bcast(far[8:16, 62:63]), bcast(far[8:16, 63:64]))
@@ -352,15 +396,15 @@
             value = value + lroll(value, 32)
             return value + lroll(value, 64)
 
-        p0_z, p1_z, p2_z = (repeat(flow_cols[i * 8:i * 8 + 8, :], 0) for i in range(3))
-        p1_m, cs_m, cn_m = (repeat(flow_cols[i * 8:i * 8 + 8, :], 32) for i in (1, 3, 4))
+        p1_z, p1_m, p2_z, p0_z = (repeat(flow_cols[0:8, :], offset) for offset in (0, 32, 64, 96))
+        corner_m = repeat(flow_cols[8:16, :], 32)
         k_lane = (pair & (K - 1)).astype(F32)
         lim = functools.partial(jnp.minimum, p1_lev)
         c = coefficients(
             face(k_lane, lim(jnp.where(even, p2_lev, p0_lev)), p1_z),
             face(k_lane, lim(jnp.where(even, p0_lev, p2_lev)), jnp.where(even, p0_z, p2_z)),
             face(k_lane, lim(up_one(p1_lev, cn_lev)), p1_m),
-            face(k_lane, lim(down_one(p1_lev, cs_lev)), down_one(p1_m, cs_m)),
+            face(k_lane, lim(down_one(p1_lev, cs_lev)), down_one(p1_m, corner_m)),
         )
         for v in range(2):
             a = slice(v * 8, v * 8 + 8)
@@ -374,42 +418,38 @@
         def turn(value, corner):
             return jnp.where(last_lane, corner, lroll(value, 127)), jnp.where(first_lane, corner, lroll(value, 1))
 
-        for north_side in range(2):
+        def ring_of(north_side, octet):
             at = 0 if north_side else 7
             corner = corner_n if north_side else corner_s
-            corner_z = flow_cols[32:40, :] if north_side else flow_cols[24:32, :]
-            base = 3 * K if north_side else 0
+            base = 24 if north_side else 0
             r_lev = rows[north_side, NT:NT + 8, :]
             r_in = rows_out[1 - north_side, NT:NT + 8, :]
             r_out = rows[2 + north_side, NT:NT + 8, :]
             r_e, r_w = turn(r_lev, lroll(bcast(corner[8 + at:9 + at, :]), 65))
-            for octet in range(2):
-                k_row = (row + 8 * octet).astype(F32)
-                z = flow_rows[base + octet * 8:base + octet * 8 + 8, :]
-                m = flow_rows[base + K + octet * 8:base + K + octet * 8 + 8, :]
-                _, zw = turn(z, corner_of(corner_z, at, octet * 8))
-                lim_in, lim_out = jnp.minimum(r_lev, r_in), jnp.minimum(r_lev, r_out)
-                if north_side:
-                    inner = zm[pl.ds(K * 8 + octet * 64 + 7, 8, stride=8), :]
-                    fn, fs = face(k_row, lim_out, m), face(k_row, lim_in, inner)
-                else:
-                    outer = flow_rows[2 * K + octet * 8:2 * K + octet * 8 + 8, :]
-                    fn, fs = face(k_row, lim_in, m), face(k_row, lim_out, outer)
-                c = coefficients(face(k_row, jnp.minimum(r_lev, r_e), z), face(k_row, jnp.minimum(r_lev, r_w), zw), fn, fs)
-                for f in range(NF):
-                    v, p, u = f // 4, (f % 4) * K + octet * 8, (f * K + octet * 8)
-                    a = slice(u, u + 8)
-                    q, inner, outer = rows[north_side, a, :], rows_out[1 - north_side, a, :], rows[2 + north_side, a, :]
-                    qe, qw = turn(q, corner_of(corner[v * 8:v * 8 + 8, :], at, p))
-                    qn, qs = (outer, inner) if north_side else (inner, outer)
-                    ring_rows[north_side, a, :] = combine(c, q, qe, qw, qn, qs)
-
-        def advance(k, carry):
+            k_row = (row + 8 * octet).astype(F32)
+            z = flow_rows[octet, base:base + 8, :]
+            m = flow_rows[octet, base + 8:base + 16, :]
+            _, zw = turn(z, corner_of(flow_cols[8:16, :], at, octet * 8))
+            lim_in, lim_out = jnp.minimum(r_lev, r_in), jnp.minimum(r_lev, r_out)
+            if north_side:
+                fn, fs = face(k_row, lim_out, m), face(k_row, lim_in, flow_rows_out[octet, 8:16, :])
+            else:
+                fn, fs = face(k_row, lim_in, m), face(k_row, lim_out, flow_rows[octet, 16:24, :])
+            c = coefficients(face(k_row, jnp.minimum(r_lev, r_e), z), face(k_row, jnp.minimum(r_lev, r_w), zw), fn, fs)
+            for f in range(NF):
+                v, p, u = f // 4, (f % 4) * K + octet * 8, (f * K + octet * 8)
+                a = slice(u, u + 8)
+                q, inner, outer = rows[north_side, a, :], rows_out[1 - north_side, a, :], rows[2 + north_side, a, :]
+                qe, qw = turn(q, corner_of(corner[v * 8:v * 8 + 8, :], at, p))
+                qn, qs = (outer, inner) if north_side else (inner, outer)
+                ring_rows[north_side, a, :] = combine(c, q, qe, qw, qn, qs)
+
+        def advance(octet, k, carry):
             level = lax.convert_element_type(k, F32)
             z, m = zm[tile(k), :], zm[tile(K + k), :]
-            side = lroll(flow_cols[8:16, :], 2 * k + 1)
+            side = lroll(flow_cols[0:8, :], 2 * k + 1)
             zw = jnp.where(first_lane, side, lroll(z, 1))
-            ms = jnp.where(first_row, bcast(flow_rows[pl.ds(K + k, 1), :]), sroll(m, 1))
+            ms = jnp.where(first_row, bcast(flow_rows[octet, pl.ds(k + 8 - octet * 8, 1), :]), sroll(m, 1))
             fe, fw, fn, fs = face(level, lim_e, z), face(level, lim_w, zw), face(level, lim_n, m), face(level, lim_s, ms)
             div[tile(k), :] = (fe - fw) + (fn - fs)
             c = coefficients(fe, fw, fn, fs)
@@ -420,8 +460,23 @@
                 rhs[tile(f * K + k), :] = q
             return carry
 
-        lax.fori_loop(0, K, advance, 0)
-        across(Z_DIFF, 1).wait_recv()
+        for octet in range(2):
+            if octet:
+                share_rows(1)
+
+            @pl.when(has_s)
+            def _(octet=octet):
+                flow_s(octet).wait_recv()
+
+            @pl.when(has_n)
+            def _(octet=octet):
+                flow_n(octet).wait_recv()
+
+            ring_of(0, octet)
+            ring_of(1, octet)
+            lax.fori_loop(octet * 8, octet * 8 + 8, functools.partial(advance, octet), 0)
+        send_diff[0].wait_recv()
+        part_of(1 - own, peer).wait_recv()
 
         def eliminate(i, carry):
             total, up_below, down_below, ratio_below, below = carry
@@ -460,19 +515,38 @@
 
     @pl.when(has_n)
     def _():
-        for copy in (near_s, far_s, edge_s):
+        near_s.wait_send()
+        edge_s.wait_send()
+
+    @pl.when(has_s)
+    def _():
+        near_n.wait_send()
+        edge_n.wait_send()
+
+    @pl.when(has_n & (sect != 0))
+    def _():
+        for copy in (far_s, flow_s(0), flow_s(1)):
             copy.wait_send()
 
-    @pl.when(has_s)
-    def _():
-        for copy in (near_n, far_n, edge_n):
+    @pl.when(has_s & (sect != 0))
+    def _():
+        for copy in (far_n, flow_n(0), flow_n(1)):
             copy.wait_send()
 
     @pl.when(sect == 0)
     def _():
-        for slot in range(N_Z):
-            for peer in range(1, n_sect):
-                across(slot, peer).wait_send()
+        for field in range(2):
+            for c in range(NC):
+                speed(field, c).wait_send()
+            part_of(field, field + 1).wait_send()
+        for copy in send_cols + send_diff:
+            copy.wait_send()
+
+    @pl.when(sect != 0)
+    def _():
+        for c in range(NC):
+            speed_on(sect - 1, c, 3 - sect).wait_send()
+        part_of(sect - 1, 3 - sect).wait_send()
 
 
 def solution(mesh):
@@ -497,9 +571,10 @@
                 vmem((16, 128), F32),
                 vmem((16, 128), F32),
                 vmem((2 * K * 8, 128), F32),
-                vmem((5 * K, 128), F32),
-                vmem((40, 128), F32),
-                vmem((40, 128), F32),
+                vmem((2, 40, 128), F32),
+                vmem((2, 40, 128), F32),
+                vmem((16, 128), F32),
+                vmem((16, 128), F32),
                 vmem((K * 8, 128), F32),
                 vmem((NT * 8, 128), F32),
                 vmem((K * 8, 128), F32),
@@ -509,7 +584,8 @@
                 pltpu.SemaphoreType.DMA,
                 pltpu.SemaphoreType.DMA((N_HALO,)),
                 pltpu.SemaphoreType.DMA((N_HALO,)),
-                pltpu.SemaphoreType.DMA((n_sect - 1, N_Z)),
+                pltpu.SemaphoreType.DMA((N_Z,)),
+                pltpu.SemaphoreType.DMA((n_sect - 1, 2)),
                 pltpu.SemaphoreType.DMA((N_Z,)),
             ],
             compiler_params=pltpu.CompilerParams(collective_id=0, has_side_effects=True),

time: 39.5 us -> 36 us (0.911)
  the two profiles are of different devices: /device:TPU:1 before, /device:TPU:342 now
where the time goes in v2:
time: 36 us; the launch traced here: 35.8 us
  Pallas kernels  34 us (94%)
  local copies, waits for them, and re-layouts  1.77 us (5%)
    pallas_call x1, Pallas kernels, on_device(): pl.pallas_call(functools.partial(kernel, n_sect, n_lon, n_lat), out_shape...  34 us
    unnamed x1, local copies, waits for them, and re-layouts  1.77 us

profile of v2, /device:TPU:342, one launch (start us, length us, event | category | flops | bytes accessed | tf_op | source)
XLA Modules:
  0.0 35.8 jit_solution(18029587338835201945)
XLA Ops:
  0.0 34.0 %shard_map.28 = f32[768,128]{1,0:T(8,128)} custom-call(f32[768,128]{1,0:T(8,128)} %bitcast.3, s32[8,128]{1,0:T(8,128)} %lev_ref.1), custom_call_target="tpu_custom_call" | custom-call | tf_op jit(solution)/shard_map/pallas_call | solution.py:557
  34.0 1.8 %copy.4 = f32[1,6,16,8,128]{4,3,2,1,0:T(8,128)} copy(f32[1,6,16,8,128]{4,3,2,1,0:T(8,128)} %bitcast.2) | data formatting | bytes 786432

commit v3 on v2

--- a/solution.py
+++ b/solution.py
@@ -54,9 +54,9 @@
     return (c0 * q + (ce * qe + cw * qw)) + (cn * qn + cs * qs)
 
 
-def kernel(n_sect, n_lon, n_lat, x_hbm, lev_ref, out,
-           x, cols, cols_w, cols_e, rows_out, rows, near, far, corner_s, corner_n,
-           zm, flow_rows, flow_rows_out, flow_cols, flow_cols_out, diff, rhs, div, ratio, ring_cols, ring_rows,
+def kernel(n_sect, n_lon, n_lat, x_hbm, lev_hbm, out,
+           x, lev_ref, cols, cols_w, cols_e, rows_out, rows, near, far, corner_s, corner_n,
+           zm, flow_rows, flow_rows_out, flow_cols, flow_cols_out, diff, rhs, div, ratio, ring_cols, ring_rows, shifted, turned,
            in_sem, send_sem, recv_sem, zsend_sem, zsend2_sem, zrecv_sem):
     sect = lax.axis_index("sect")
     lon = lax.axis_index("lon")
@@ -80,8 +80,10 @@
     def _():
         pl.semaphore_signal(barrier, inc=1, device_id={"lat": lat + 1}, device_id_type=MESH)
 
-    load = pltpu.make_async_copy(x_hbm, x, in_sem)
+    load = pltpu.make_async_copy(x_hbm, x, in_sem.at[0])
     load.start()
+    load_lev = pltpu.make_async_copy(lev_hbm, lev_ref, in_sem.at[1])
+    load_lev.start()
 
     lane = lax.broadcasted_iota(jnp.int32, (8, 128), 1)
     row = lax.broadcasted_iota(jnp.int32, (8, 128), 0)
@@ -90,7 +92,6 @@
     pair_b = 63 - (jnp.where(even, (lane + 126) >> 1, (lane + 1) >> 1) & 63)
     first_lane, last_lane = lane == 0, lane == 127
     first_row, last_row = row == 0, row == 7
-    lev = lev_ref[...].astype(F32)
     zero = jnp.zeros((8, 128), F32)
 
     def bcast(value):
@@ -110,7 +111,9 @@
         corner_n[...] = jnp.zeros((16, 128), F32)
         flow_rows[:, 24:40, :] = jnp.zeros((2, 16, 128), F32)
 
+    load_lev.wait()
     load.wait()
+    lev = lev_ref[...].astype(F32)
 
     def pack(acc, value, turn, p):
         a, b = acc
@@ -216,6 +219,14 @@
     @pl.when(has_s & (sect != 0))
     def _():
         far_n.start()
+
+    own, peer = sect - 1, 3 - sect
+
+    @pl.when(sect != 0)
+    def _():
+        for c in range(NC):
+            speed_on(own, c, peer).wait_recv()
+            speed_on(own, c, peer).start()
 
     from_w.wait_recv()
     from_e.wait_recv()
@@ -343,12 +354,20 @@
 
     @pl.when(sect != 0)
     def _():
-        own, peer = sect - 1, 3 - sect
-        for c in range(NC):
-            speed_on(own, c, peer).wait_recv()
-            speed_on(own, c, peer).start()
-        part_of(own, peer).wait_recv()
-        part_of(own, peer).start()
+        def corner_of(value, at, p):
+            return pltpu.roll(bcast(value[at:at + 1, :]), 2 * p + 1, 1, stride=2, stride_axis=0)
+
+        def turn(value, corner):
+            return jnp.where(last_lane, corner, lroll(value, 127)), jnp.where(first_lane, corner, lroll(value, 1))
+
+        def shift(k, carry):
+            for f in range(NF):
+                q = x[tile(f * K + k), :]
+                for i, value in enumerate(neighbours(q, f, k, near, rows.at[0], rows.at[1])):
+                    shifted[i, tile(f * K + k), :] = value
+            return carry
+
+        lax.fori_loop(0, K, shift, 0)
 
         @pl.when(has_s)
         def _():
@@ -359,6 +378,14 @@
         def _():
             far_n.wait_recv()
             edge_n.wait_recv()
+
+        for north_side in range(2):
+            corner = corner_n if north_side else corner_s
+            for u in range(NT // 8):
+                v, p, a = u // 8, (u * 8) % 64, slice(u * 8, u * 8 + 8)
+                qe, qw = turn(rows[north_side, a, :], corner_of(corner[v * 8:v * 8 + 8, :], 0 if north_side else 7, p))
+                turned[north_side, 0, a, :] = qe
+                turned[north_side, 1, a, :] = qw
 
         def share_rows(octet):
             for c in range(octet * NC // 2, (octet + 1) * NC // 2):
@@ -375,6 +402,9 @@
                 flow_n(octet).start()
 
         share_rows(0)
+        part_of(own, peer).wait_recv()
+        part_of(own, peer).start()
+        share_rows(1)
         send_cols[0].wait_recv()
 
         p1_lev = jnp.where(even, bcast(near[8:16, 62:63]), bcast(near[8:16, 63:64]))
@@ -411,12 +441,6 @@
             p0, p1, p2 = cols[a, :], near[a, :], far[a, :]
             ring_cols[a, :] = combine(c, p1, jnp.where(even, p2, p0), jnp.where(even, p0, p2),
                                       up_one(p1, corner_n[a, :]), down_one(p1, corner_s[a, :]))
-
-        def corner_of(value, at, p):
-            return pltpu.roll(bcast(value[at:at + 1, :]), 2 * p + 1, 1, stride=2, stride_axis=0)
-
-        def turn(value, corner):
-            return jnp.where(last_lane, corner, lroll(value, 127)), jnp.where(first_lane, corner, lroll(value, 1))
 
         def ring_of(north_side, octet):
             at = 0 if north_side else 7
@@ -437,10 +461,9 @@
                 fn, fs = face(k_row, lim_in, m), face(k_row, lim_out, flow_rows[octet, 16:24, :])
             c = coefficients(face(k_row, jnp.minimum(r_lev, r_e), z), face(k_row, jnp.minimum(r_lev, r_w), zw), fn, fs)
             for f in range(NF):
-                v, p, u = f // 4, (f % 4) * K + octet * 8, (f * K + octet * 8)
-                a = slice(u, u + 8)
+                a = slice(f * K + octet * 8, f * K + octet * 8 + 8)
                 q, inner, outer = rows[north_side, a, :], rows_out[1 - north_side, a, :], rows[2 + north_side, a, :]
-                qe, qw = turn(q, corner_of(corner[v * 8:v * 8 + 8, :], at, p))
+                qe, qw = turned[north_side, 0, a, :], turned[north_side, 1, a, :]
                 qn, qs = (outer, inner) if north_side else (inner, outer)
                 ring_rows[north_side, a, :] = combine(c, q, qe, qw, qn, qs)
 
@@ -455,15 +478,12 @@
             c = coefficients(fe, fw, fn, fs)
             for f in range(NF):
                 q = x[tile(f * K + k), :]
-                q = combine(c, q, *neighbours(q, f, k, near, rows.at[0], rows.at[1]))
+                q = combine(c, q, *(shifted[i, tile(f * K + k), :] for i in range(4)))
                 q = combine(c, q, *neighbours(q, f, k, ring_cols, ring_rows.at[0], ring_rows.at[1]))
                 rhs[tile(f * K + k), :] = q
             return carry
 
         for octet in range(2):
-            if octet:
-                share_rows(1)
-
             @pl.when(has_s)
             def _(octet=octet):
                 flow_s(octet).wait_recv()
@@ -556,11 +576,12 @@
         vmem = pltpu.VMEM
         result = pl.pallas_call(
             functools.partial(kernel, n_sect, n_lon, n_lat),
-            out_shape=jax.ShapeDtypeStruct((NT * 8, 128), F32),
-            in_specs=[pl.BlockSpec(memory_space=pl.ANY), pl.BlockSpec(memory_space=pltpu.VMEM)],
+            out_shape=pltpu.VMEM((NT * 8, 128), F32),
+            in_specs=[pl.BlockSpec(memory_space=pl.ANY)] * 2,
             out_specs=pl.BlockSpec(memory_space=pltpu.VMEM),
             scratch_shapes=[
                 vmem((NT * 8, 128), F32),
+                vmem((8, 128), jnp.int32),
                 vmem((32, 128), F32),
                 vmem((32, 128), F32),
                 vmem((32, 128), F32),
@@ -581,7 +602,9 @@
                 vmem((K * 8, 128), F32),
                 vmem((16, 128), F32),
                 vmem((2, NT, 128), F32),
-                pltpu.SemaphoreType.DMA,
+                vmem((4, NT * 8, 128), F32),
+                vmem((2, 2, NT, 128), F32),
+                pltpu.SemaphoreType.DMA((2,)),
                 pltpu.SemaphoreType.DMA((N_HALO,)),
                 pltpu.SemaphoreType.DMA((N_HALO,)),
                 pltpu.SemaphoreType.DMA((N_Z,)),

time: 36 us -> 31.2 us (0.87)
  the two profiles are of different devices: /device:TPU:342 before, /device:TPU:468 now
where the time goes in v3:
time: 31.2 us; the launch traced here: 31.1 us
  Pallas kernels  30.3 us (97%)
  local copies, waits for them, and re-layouts  0.75 us (2%)
    pallas_call x1, Pallas kernels, on_device(): pl.pallas_call(functools.partial(kernel, n_sect, n_lon, n_lat), out_shape...  30.3 us
    unnamed x1, local copies, waits for them, and re-layouts  0.75 us

profile of v3, /device:TPU:468, one launch (start us, length us, event | category | flops | bytes accessed | tf_op | source)
XLA Modules:
  0.0 31.1 jit_solution(17486636554800545977)
XLA Ops:
  0.0 30.3 %shard_map.28 = f32[768,128]{1,0:T(8,128)S(1)} custom-call(f32[768,128]{1,0:T(8,128)} %bitcast.3, s32[8,128]{1,0:T(8,128)} %lev_hbm.1), custom_call_target="tpu_custom_call" | custom-call | tf_op jit(solution)/shard_map/pallas_call | solution.py:577
  30.3 0.7 %copy.4 = f32[1,6,16,8,128]{4,3,2,1,0:T(8,128)} copy(f32[1,6,16,8,128]{4,3,2,1,0:T(8,128)S(1)} %bitcast.2) | data formatting | bytes 786432

commit v4 on v3

--- a/solution.py
+++ b/solution.py
@@ -19,9 +19,13 @@
 N_HALO = 12
 CH = 2
 NC = K // CH
-DV = 3
-Z_PART, Z_COL, Z_DIFF = 2 * NC, 2 * NC + 2, 2 * NC + 3
-N_Z = 2 * NC + 4
+Z_COL, Z_DIFF = 2 * NC, 2 * NC + 1
+N_Z = 2 * NC + 2
+DEPTH = 4
+VIA_FIRST = 2
+VIA_SECOND = 3
+(E, W, N, S, FIRST, SECOND, GO) = range(7)
+MID = 2
 
 
 def tile(t):
@@ -57,7 +61,7 @@
 def kernel(n_sect, n_lon, n_lat, x_hbm, lev_hbm, out,
            x, lev_ref, cols, cols_w, cols_e, rows_out, rows, near, far, corner_s, corner_n,
            zm, flow_rows, flow_rows_out, flow_cols, flow_cols_out, diff, rhs, div, ratio, ring_cols, ring_rows, shifted, turned,
-           in_sem, send_sem, recv_sem, zsend_sem, zsend2_sem, zrecv_sem):
+           in_sem, send_sem, recv_sem, zsend_sem, zrecv_sem, ready):
     sect = lax.axis_index("sect")
     lon = lax.axis_index("lon")
     lat = lax.axis_index("lat")
@@ -66,19 +70,36 @@
     has_s = lat > 0
     has_n = lat < n_lat - 1
 
+    place = lax.rem(lon // 2, DEPTH)
+    to_first, to_second = place < VIA_SECOND, place >= VIA_FIRST
+    onward = (sect == 1) & jnp.logical_not(to_second)
+    passes_on = onward | ((sect == 2) & jnp.logical_not(to_first))
+    paired = jnp.logical_not(to_first & to_second)
+
+    run, half = 2 * DEPTH, n_lat // 2
+    end, head = lax.rem(lon, run) == run - 1, lax.rem(lon, run) == 0
+    to = ({"lon": east}, {"lon": west}, {"lat": lat + 1}, {"lat": lat - 1}, {"sect": 1}, {"sect": 2})
+    announces = (jnp.logical_not(end), head, has_n & ((lat < half) | (lat == n_lat - 2)), has_s & ((lat > half) | (lat == 1)),
+                 (sect == 0) & to_first, ((sect == 0) & to_second) | ((sect == 1) & paired))
+    hears = (end, jnp.logical_not(head), has_n & ((lat >= half) | (lat == 0)), has_s & ((lat <= half) | (lat == n_lat - 1)))
+    hears_sect = ((sect == 1) & to_first, (sect == 2) & to_second, (sect == 2) & paired)
+
+    def signal(sem, where):
+        pl.semaphore_signal(sem, inc=1, device_id=where, device_id_type=MESH)
+
+    mid = (sect == 0) & (place == MID)
+    held = (sect == 0) & (place != MID)
+
     barrier = pltpu.get_barrier_semaphore()
-    for step in range(1, n_sect):
-        pl.semaphore_signal(barrier, inc=1, device_id={"sect": lax.rem(sect + step, n_sect)}, device_id_type=MESH)
-    for side in (east, west):
-        pl.semaphore_signal(barrier, inc=1, device_id={"lon": side}, device_id_type=MESH)
-
-    @pl.when(has_s)
-    def _():
-        pl.semaphore_signal(barrier, inc=1, device_id={"lat": lat - 1}, device_id_type=MESH)
-
-    @pl.when(has_n)
-    def _():
-        pl.semaphore_signal(barrier, inc=1, device_id={"lat": lat + 1}, device_id_type=MESH)
+
+    @pl.when(held)
+    def _():
+        signal(barrier, {"lon": lon + 2 * (MID - place)})
+
+    for side in range(6):
+        @pl.when(announces[side])
+        def _(side=side):
+            signal(barrier, to[side])
 
     load = pltpu.make_async_copy(x_hbm, x, in_sem.at[0])
     load.start()
@@ -96,6 +117,23 @@
 
     def bcast(value):
         return jnp.broadcast_to(value, (8, 128))
+
+    pl.semaphore_wait(barrier, sum(heard.astype(jnp.int32) for heard in hears + hears_sect) + jnp.where(mid, DEPTH - 1, 0))
+    for side, back in ((E, W), (W, E), (N, S), (S, N)):
+        @pl.when(hears[side])
+        def _(side=side, back=back):
+            signal(ready.at[back], to[side])
+
+    for heard, slot, lower in ((hears_sect[0], FIRST, 0), (hears_sect[1], SECOND, 0),
+                               ((sect == 2) & jnp.logical_not(to_second), SECOND, 1)):
+        @pl.when(heard)
+        def _(slot=slot, lower=lower):
+            signal(ready.at[slot], {"sect": lower})
+
+    def await_ready(side, only=True):
+        @pl.when(announces[side] & only)
+        def _():
+            pl.semaphore_wait(ready.at[side], 1)
 
     @pl.when(jnp.logical_not(has_s))
     def _():
@@ -131,7 +169,7 @@
                 a1, b1 = pack((a1, b1), value, 127 - 2 * p, p)
         return a0, a1, b0, b1
 
-    a0, a1, b0, b1 = lax.fori_loop(0, K, pack_level, (zero,) * 4)
+    a0, a1, b0, b1 = lax.fori_loop(0, K, pack_level, (zero,) * 4, unroll=4)
     a1, b1 = pack((a1, b1), lev, 63, 32)
     for i, value in enumerate((a0, a1, b0, b1)):
         cols[i * 8:i * 8 + 8, :] = value
@@ -141,11 +179,9 @@
             rows_out[i, tile(u), :] = x[pl.ds(u * 64 + r, 8, stride=8), :]
         return carry
 
-    lax.fori_loop(0, NT // 8, pack_rows, 0)
+    lax.fori_loop(0, NT // 8, pack_rows, 0, unroll=4)
     for i, r in enumerate((7, 0, 6, 1)):
         rows_out[i, NT:NT + 8, :] = bcast(lev[r:r + 1, :])
-
-    pl.semaphore_wait(barrier, n_sect + 1 + has_s.astype(jnp.int32) + has_n.astype(jnp.int32))
 
     def remote(src, dst, send, recv, to):
         return pltpu.make_async_remote_copy(src_ref=src, dst_ref=dst, send_sem=send, recv_sem=recv, device_id=to,
@@ -176,27 +212,43 @@
     def rows_of(ref, start, size):
         return ref.at[pl.ds(pl.multiple_of(start * 8, 8), size * 8)]
 
-    def speed(field, c):
-        return across(rows_of(x_hbm, field * K + c * CH, CH), rows_of(zm, field * K + c * CH, CH), field * NC + c, field + 1)
-
-    def speed_on(field, c, peer):
-        part = rows_of(zm, field * K + c * CH, CH)
-        return across(part, part, field * NC + c, peer)
-
-    def part_of(field, peer):
-        part = rows_of(diff, field * DV, DV)
-        return across(part, part, Z_PART + field, peer)
-
-    def both(slot, src, dst):
-        return [remote(src, dst, zsend2_sem.at[peer - 1, slot - Z_COL], zrecv_sem.at[slot], {"sect": peer})
-                for peer in range(1, n_sect)]
-
-    send_cols = both(Z_COL, flow_cols_out, flow_cols)
-    rest = slice(2 * DV * 8, K * 8)
-    send_diff = both(Z_DIFF, diff.at[rest], diff.at[rest])
-
+    peer = 3 - sect
+
+    def chunk(field, c, target, relayed=False):
+        part = field * K + c * CH
+        slot = field * NC + c
+        src = rows_of(zm if relayed else x_hbm, part, CH)
+        return remote(src, rows_of(zm, part, CH), zsend_sem.at[0 if relayed else target - 1, slot], zrecv_sem.at[slot],
+                      {"sect": target})
+
+    def send_cols(target, relayed=False):
+        return remote(flow_cols if relayed else flow_cols_out, flow_cols, zsend_sem.at[0 if relayed else target - 1, Z_COL],
+                      zrecv_sem.at[Z_COL], {"sect": target})
+
+    def send_diff(target, relayed=False):
+        return remote(diff, diff, zsend_sem.at[0 if relayed else target - 1, Z_DIFF], zrecv_sem.at[Z_DIFF], {"sect": target})
+
+    def to_tracers(act, targets, *copies):
+        for target in targets:
+            @pl.when((to_first, to_second)[target - 1])
+            def _(target=target):
+                for make in copies:
+                    act(make(target))
+
+    def start(copy):
+        copy.start()
+
+    def wait_send(copy):
+        copy.wait_send()
+
+    chunks = [functools.partial(chunk, field, c) for c in range(NC) for field in range(2)]
+
+    await_ready(E)
     from_w.start()
+    await_ready(W)
     from_e.start()
+    await_ready(N)
+    await_ready(S)
 
     @pl.when(has_n)
     def _():
@@ -208,9 +260,8 @@
 
     @pl.when(sect == 0)
     def _():
-        for c in range(NC):
-            for field in range(2):
-                speed(field, c).start()
+        await_ready(FIRST)
+        to_tracers(start, (1,), *chunks)
 
     @pl.when(has_n & (sect != 0))
     def _():
@@ -220,13 +271,13 @@
     def _():
         far_n.start()
 
-    own, peer = sect - 1, 3 - sect
-
-    @pl.when(sect != 0)
-    def _():
-        for c in range(NC):
-            speed_on(own, c, peer).wait_recv()
-            speed_on(own, c, peer).start()
+    await_ready(SECOND, onward)
+
+    @pl.when(passes_on)
+    def _():
+        for make in chunks:
+            make(peer, True).wait_recv()
+            make(peer, True).start()
 
     from_w.wait_recv()
     from_e.wait_recv()
@@ -299,10 +350,7 @@
             diff[tile(k), :] = mixing
             return new
 
-        lax.fori_loop(0, K, warm, zero)
-
-        for field in range(2):
-            part_of(field, field + 1).start()
+        lax.fori_loop(0, K, warm, zero, unroll=4)
 
         @pl.when(has_s)
         def _():
@@ -315,8 +363,18 @@
         flow_cols_out[0:8, :] = jnp.where(
             lane >= 64, near[0:8, :], jnp.where(lane >= 32, lroll(far[0:8, :], 64), lroll(cols[0:8, :], 32)))
         flow_cols_out[8:16, :] = jnp.where(first_row, corner_n[0:8, :], corner_s[0:8, :])
-        for copy in send_cols + send_diff:
-            copy.start()
+        to_tracers(start, (1,), send_cols)
+
+        @pl.when(mid)
+        def _():
+            send_diff(1).start()
+
+        await_ready(SECOND)
+        to_tracers(start, (2,), *chunks, send_cols)
+
+        @pl.when(mid)
+        def _():
+            send_diff(2).start()
 
         def move(k, sums):
             level = lax.convert_element_type(k, F32)
@@ -342,7 +400,7 @@
                 face(level, lim_n, m) - face(level, lim_s, ms[3]))
             return here, at_e, at_n
 
-        lax.fori_loop(0, K, move, (zero,) * 3)
+        lax.fori_loop(0, K, move, (zero,) * 3, unroll=2)
 
         def rise(i, total):
             k = K - 1 - i
@@ -350,7 +408,20 @@
             out[tile(4 * K + k), :] = jnp.where(k > 0, -total, 0.0)
             return total
 
-        lax.fori_loop(0, K, rise, zero)
+        lax.fori_loop(0, K, rise, zero, unroll=4)
+
+        @pl.when(mid)
+        def _():
+            for target, others in ((1, range(MID)), (2, range(MID + 1, DEPTH))):
+                for make in chunks:
+                    make(target).wait_send()
+                for other in others:
+                    signal(ready.at[GO], {"lon": lon + 2 * (other - MID)})
+
+        @pl.when(held)
+        def _():
+            pl.semaphore_wait(ready.at[GO], 1)
+            to_tracers(start, (1, 2), send_diff)
 
     @pl.when(sect != 0)
     def _():
@@ -367,8 +438,27 @@
                     shifted[i, tile(f * K + k), :] = value
             return carry
 
-        lax.fori_loop(0, K, shift, 0)
-
+        lax.fori_loop(0, K, shift, 0, unroll=2)
+
+        def share_rows(octet):
+            @pl.when(jnp.logical_not(passes_on))
+            def _():
+                for make in chunks[octet * NC:(octet + 1) * NC]:
+                    make(1).wait_recv()
+
+            for i, (field, r) in enumerate(((0, 7), (1, 7), (1, 6), (0, 0), (1, 0))):
+                flow_rows_out[octet, i * 8:i * 8 + 8, :] = zm[pl.ds((field * K + octet * 8) * 8 + r, 8, stride=8), :]
+
+            @pl.when(has_n)
+            def _():
+                flow_s(octet).start()
+
+            @pl.when(has_s)
+            def _():
+                flow_n(octet).start()
+
+        share_rows(0)
+        share_rows(1)
         @pl.when(has_s)
         def _():
             far_s.wait_recv()
@@ -387,25 +477,12 @@
                 turned[north_side, 0, a, :] = qe
                 turned[north_side, 1, a, :] = qw
 
-        def share_rows(octet):
-            for c in range(octet * NC // 2, (octet + 1) * NC // 2):
-                speed_on(1 - own, c, peer).wait_recv()
-            for i, (field, r) in enumerate(((0, 7), (1, 7), (1, 6), (0, 0), (1, 0))):
-                flow_rows_out[octet, i * 8:i * 8 + 8, :] = zm[pl.ds((field * K + octet * 8) * 8 + r, 8, stride=8), :]
-
-            @pl.when(has_n)
-            def _():
-                flow_s(octet).start()
-
-            @pl.when(has_s)
-            def _():
-                flow_n(octet).start()
-
-        share_rows(0)
-        part_of(own, peer).wait_recv()
-        part_of(own, peer).start()
-        share_rows(1)
-        send_cols[0].wait_recv()
+        send_cols(1).wait_recv()
+
+        @pl.when(passes_on)
+        def _():
+            send_cols(peer, True).start()
+
 
         p1_lev = jnp.where(even, bcast(near[8:16, 62:63]), bcast(near[8:16, 63:64]))
         p2_lev = jnp.where(even, bcast(far[8:16, 62:63]), bcast(far[8:16, 63:64]))
@@ -494,9 +571,14 @@
 
             ring_of(0, octet)
             ring_of(1, octet)
-            lax.fori_loop(octet * 8, octet * 8 + 8, functools.partial(advance, octet), 0)
-        send_diff[0].wait_recv()
-        part_of(1 - own, peer).wait_recv()
+            lax.fori_loop(octet * 8, octet * 8 + 8, functools.partial(advance, octet), 0, unroll=4)
+
+        send_diff(1).wait_recv()
+
+        @pl.when(passes_on)
+        def _():
+            send_diff(peer, True).start()
+
 
         def eliminate(i, carry):
             total, up_below, down_below, ratio_below, below = carry
@@ -516,7 +598,7 @@
                 values.append(value)
             return total, up, down, here, tuple(values)
 
-        lax.fori_loop(0, K, eliminate, (zero,) * 4 + ((zero,) * NF,))
+        lax.fori_loop(0, K, eliminate, (zero,) * 4 + ((zero,) * NF,), unroll=4)
 
         def settle(k, above):
             level = lax.convert_element_type(k, F32)
@@ -528,7 +610,7 @@
                 values.append(value)
             return tuple(values)
 
-        lax.fori_loop(0, K, settle, (zero,) * NF)
+        lax.fori_loop(0, K, settle, (zero,) * NF, unroll=4)
 
     from_w.wait_send()
     from_e.wait_send()
@@ -555,18 +637,16 @@
 
     @pl.when(sect == 0)
     def _():
-        for field in range(2):
-            for c in range(NC):
-                speed(field, c).wait_send()
-            part_of(field, field + 1).wait_send()
-        for copy in send_cols + send_diff:
-            copy.wait_send()
-
-    @pl.when(sect != 0)
-    def _():
-        for c in range(NC):
-            speed_on(sect - 1, c, 3 - sect).wait_send()
-        part_of(sect - 1, 3 - sect).wait_send()
+        @pl.when(held)
+        def _():
+            to_tracers(wait_send, (1, 2), *chunks)
+
+        to_tracers(wait_send, (1, 2), send_cols, send_diff)
+
+    @pl.when(passes_on)
+    def _():
+        for make in (*chunks, send_cols, send_diff):
+            make(peer, True).wait_send()
 
 
 def solution(mesh):
@@ -607,9 +687,9 @@
                 pltpu.SemaphoreType.DMA((2,)),
                 pltpu.SemaphoreType.DMA((N_HALO,)),
                 pltpu.SemaphoreType.DMA((N_HALO,)),
+                pltpu.SemaphoreType.DMA((n_sect - 1, N_Z)),
                 pltpu.SemaphoreType.DMA((N_Z,)),
-                pltpu.SemaphoreType.DMA((n_sect - 1, 2)),
-                pltpu.SemaphoreType.DMA((N_Z,)),
+                pltpu.SemaphoreType.REGULAR((7,)),
             ],
             compiler_params=pltpu.CompilerParams(collective_id=0, has_side_effects=True),
         )(fields.reshape(NT * 8, 128), levels)

time: 31.2 us -> 28.8 us (0.923)
  the two profiles are of different devices: /device:TPU:468 before, /device:TPU:600 now
where the time goes in v4:
time: 28.8 us; the launch traced here: 28.6 us
  Pallas kernels  27.9 us (97%)
  local copies, waits for them, and re-layouts  0.75 us (3%)
    pallas_call x1, Pallas kernels, on_device(): pl.pallas_call(functools.partial(kernel, n_sect, n_lon, n_lat), out_shape...  27.9 us
    unnamed x1, local copies, waits for them, and re-layouts  0.75 us

profile of v4, /device:TPU:600, one launch (start us, length us, event | category | flops | bytes accessed | tf_op | source)
XLA Modules:
  0.0 28.6 jit_solution(9343295946111463976)
XLA Ops:
  0.0 27.9 %shard_map.28 = f32[768,128]{1,0:T(8,128)S(1)} custom-call(f32[768,128]{1,0:T(8,128)} %bitcast.3, s32[8,128]{1,0:T(8,128)} %lev_hbm.1), custom_call_target="tpu_custom_call" | custom-call | tf_op jit(solution)/shard_map/pallas_call | solution.py:657
  27.9 0.7 %copy.4 = f32[1,6,16,8,128]{4,3,2,1,0:T(8,128)} copy(f32[1,6,16,8,128]{4,3,2,1,0:T(8,128)S(1)} %bitcast.2) | data formatting | bytes 786432

commit v5 on v4

--- a/solution.py
+++ b/solution.py
@@ -364,17 +364,8 @@
             lane >= 64, near[0:8, :], jnp.where(lane >= 32, lroll(far[0:8, :], 64), lroll(cols[0:8, :], 32)))
         flow_cols_out[8:16, :] = jnp.where(first_row, corner_n[0:8, :], corner_s[0:8, :])
         to_tracers(start, (1,), send_cols)
-
-        @pl.when(mid)
-        def _():
-            send_diff(1).start()
-
         await_ready(SECOND)
         to_tracers(start, (2,), *chunks, send_cols)
-
-        @pl.when(mid)
-        def _():
-            send_diff(2).start()
 
         def move(k, sums):
             level = lax.convert_element_type(k, F32)
@@ -418,10 +409,13 @@
                 for other in others:
                     signal(ready.at[GO], {"lon": lon + 2 * (other - MID)})
 
-        @pl.when(held)
-        def _():
-            pl.semaphore_wait(ready.at[GO], 1)
-            to_tracers(start, (1, 2), send_diff)
+        pl.semaphore_wait(ready.at[GO], 1)
+        to_tracers(start, (1, 2), send_diff)
+
+        @pl.when(place == 0)
+        def _():
+            send_diff(1).wait_send()
+            signal(ready.at[GO], {"lon": lon + 2 * MID})
 
     @pl.when(sect != 0)
     def _():
@@ -641,7 +635,11 @@
         def _():
             to_tracers(wait_send, (1, 2), *chunks)
 
-        to_tracers(wait_send, (1, 2), send_cols, send_diff)
+        to_tracers(wait_send, (1, 2), send_cols)
+
+        @pl.when(place != 0)
+        def _():
+            to_tracers(wait_send, (1, 2), send_diff)
 
     @pl.when(passes_on)
     def _():

time: 28.8 us -> 27.2 us (0.944)
  the two profiles are of different devices: /device:TPU:600 before, /device:TPU:128 now
where the time goes in v5:
time: 27.2 us; the launch traced here: 27 us
  Pallas kernels  26.3 us (97%)
  local copies, waits for them, and re-layouts  0.75 us (3%)
    pallas_call x1, Pallas kernels, on_device(): pl.pallas_call(functools.partial(kernel, n_sect, n_lon, n_lat), out_shape...  26.3 us
    unnamed x1, local copies, waits for them, and re-layouts  0.75 us

profile of v5, /device:TPU:128, one launch (start us, length us, event | category | flops | bytes accessed | tf_op | source)
XLA Modules:
  0.0 27.0 jit_solution(12566593248787268651)
XLA Ops:
  0.0 26.3 %shard_map.28 = f32[768,128]{1,0:T(8,128)S(1)} custom-call(f32[768,128]{1,0:T(8,128)} %bitcast.3, s32[8,128]{1,0:T(8,128)} %lev_hbm.1), custom_call_target="tpu_custom_call" | custom-call | tf_op jit(solution)/shard_map/pallas_call | solution.py:655
  26.3 0.7 %copy.4 = f32[1,6,16,8,128]{4,3,2,1,0:T(8,128)} copy(f32[1,6,16,8,128]{4,3,2,1,0:T(8,128)S(1)} %bitcast.2) | data formatting | bytes 786432

commit v6 on v5

--- a/solution.py
+++ b/solution.py
@@ -17,7 +17,7 @@
 
 (R_COL_W, R_COL_E, R_NEAR_S, R_NEAR_N, R_FAR_S, R_FAR_N, R_CORNER_S, R_CORNER_N, R_FLOW_S, R_FLOW_N) = (*range(8), 8, 10)
 N_HALO = 12
-CH = 2
+CH = 4
 NC = K // CH
 Z_COL, Z_DIFF = 2 * NC, 2 * NC + 1
 N_Z = 2 * NC + 2
@@ -73,7 +73,8 @@
     place = lax.rem(lon // 2, DEPTH)
     to_first, to_second = place < VIA_SECOND, place >= VIA_FIRST
     onward = (sect == 1) & jnp.logical_not(to_second)
-    passes_on = onward | ((sect == 2) & jnp.logical_not(to_first))
+    back = (sect == 2) & jnp.logical_not(to_first)
+    passes_on = onward | back
     paired = jnp.logical_not(to_first & to_second)
 
     run, half = 2 * DEPTH, n_lat // 2
@@ -119,16 +120,16 @@
         return jnp.broadcast_to(value, (8, 128))
 
     pl.semaphore_wait(barrier, sum(heard.astype(jnp.int32) for heard in hears + hears_sect) + jnp.where(mid, DEPTH - 1, 0))
-    for side, back in ((E, W), (W, E), (N, S), (S, N)):
-        @pl.when(hears[side])
-        def _(side=side, back=back):
-            signal(ready.at[back], to[side])
-
     for heard, slot, lower in ((hears_sect[0], FIRST, 0), (hears_sect[1], SECOND, 0),
                                ((sect == 2) & jnp.logical_not(to_second), SECOND, 1)):
         @pl.when(heard)
         def _(slot=slot, lower=lower):
             signal(ready.at[slot], {"sect": lower})
+
+    for side, slot in ((E, W), (W, E), (N, S), (S, N)):
+        @pl.when(hears[side])
+        def _(side=side, slot=slot):
+            signal(ready.at[slot], to[side])
 
     def await_ready(side, only=True):
         @pl.when(announces[side] & only)
@@ -226,7 +227,8 @@
                       zrecv_sem.at[Z_COL], {"sect": target})
 
     def send_diff(target, relayed=False):
-        return remote(diff, diff, zsend_sem.at[0 if relayed else target - 1, Z_DIFF], zrecv_sem.at[Z_DIFF], {"sect": target})
+        part = diff.at[8:K * 8]
+        return remote(part, part, zsend_sem.at[0 if relayed else target - 1, Z_DIFF], zrecv_sem.at[Z_DIFF], {"sect": target})
 
     def to_tracers(act, targets, *copies):
         for target in targets:
@@ -270,6 +272,10 @@
     @pl.when(has_s & (sect != 0))
     def _():
         far_n.start()
+
+    @pl.when(sect != 0)
+    def _():
+        diff[0:8, :] = zero
 
     await_ready(SECOND, onward)
 
@@ -365,7 +371,7 @@
         flow_cols_out[8:16, :] = jnp.where(first_row, corner_n[0:8, :], corner_s[0:8, :])
         to_tracers(start, (1,), send_cols)
         await_ready(SECOND)
-        to_tracers(start, (2,), *chunks, send_cols)
+        to_tracers(start, (2,), send_cols, *chunks)
 
         def move(k, sums):
             level = lax.convert_element_type(k, F32)
@@ -434,6 +440,29 @@
 
         lax.fori_loop(0, K, shift, 0, unroll=2)
 
+        def turn_rows():
+            @pl.when(has_s)
+            def _():
+                far_s.wait_recv()
+                edge_s.wait_recv()
+
+            @pl.when(has_n)
+            def _():
+                far_n.wait_recv()
+                edge_n.wait_recv()
+
+            for north_side in range(2):
+                corner = corner_n if north_side else corner_s
+                for u in range(NT // 8):
+                    v, p, a = u // 8, (u * 8) % 64, slice(u * 8, u * 8 + 8)
+                    qe, qw = turn(rows[north_side, a, :], corner_of(corner[v * 8:v * 8 + 8, :], 0 if north_side else 7, p))
+                    turned[north_side, 0, a, :] = qe
+                    turned[north_side, 1, a, :] = qw
+
+        @pl.when(jnp.logical_not(passes_on))
+        def _():
+            turn_rows()
+
         def share_rows(octet):
             @pl.when(jnp.logical_not(passes_on))
             def _():
@@ -453,29 +482,20 @@
 
         share_rows(0)
         share_rows(1)
-        @pl.when(has_s)
-        def _():
-            far_s.wait_recv()
-            edge_s.wait_recv()
-
-        @pl.when(has_n)
-        def _():
-            far_n.wait_recv()
-            edge_n.wait_recv()
-
-        for north_side in range(2):
-            corner = corner_n if north_side else corner_s
-            for u in range(NT // 8):
-                v, p, a = u // 8, (u * 8) % 64, slice(u * 8, u * 8 + 8)
-                qe, qw = turn(rows[north_side, a, :], corner_of(corner[v * 8:v * 8 + 8, :], 0 if north_side else 7, p))
-                turned[north_side, 0, a, :] = qe
-                turned[north_side, 1, a, :] = qw
+        @pl.when(passes_on)
+        def _():
+            turn_rows()
 
         send_cols(1).wait_recv()
 
         @pl.when(passes_on)
         def _():
             send_cols(peer, True).start()
+
+        @pl.when(back)
+        def _():
+            send_diff(peer, True).wait_recv()
+            send_diff(peer, True).start()
 
 
         p1_lev = jnp.where(even, bcast(near[8:16, 62:63]), bcast(near[8:16, 63:64]))
@@ -567,9 +587,11 @@
             ring_of(1, octet)
             lax.fori_loop(octet * 8, octet * 8 + 8, functools.partial(advance, octet), 0, unroll=4)
 
-        send_diff(1).wait_recv()
-
-        @pl.when(passes_on)
+        @pl.when(jnp.logical_not(back))
+        def _():
+            send_diff(1).wait_recv()
+
+        @pl.when(onward)
         def _():
             send_diff(peer, True).start()
 

time: 27.2 us -> 26.9 us (0.989)
  Pallas kernels: 26.3 us -> 26 us
    pallas_call x1, Pallas kernels: 26.3 us -> 26 us  [on_device(): pl.pallas_call(functools.partial(kernel, n_sect, n_lon, n_lat), out_shape...]
where the time goes in v6:
time: 26.9 us; the launch traced here: 26.7 us
  Pallas kernels  26 us (97%)
  local copies, waits for them, and re-layouts  0.75 us (3%)
    pallas_call x1, Pallas kernels, on_device(): pl.pallas_call(functools.partial(kernel, n_sect, n_lon, n_lat), out_shape...  26 us
    unnamed x1, local copies, waits for them, and re-layouts  0.75 us

profile of v6, /device:TPU:128, one launch (start us, length us, event | category | flops | bytes accessed | tf_op | source)
XLA Modules:
  0.0 26.7 jit_solution(11800336278019556467)
XLA Ops:
  0.0 26.0 %shard_map.28 = f32[768,128]{1,0:T(8,128)S(1)} custom-call(f32[768,128]{1,0:T(8,128)} %bitcast.3, s32[8,128]{1,0:T(8,128)} %lev_hbm.1), custom_call_target="tpu_custom_call" | custom-call | tf_op jit(solution)/shard_map/pallas_call | solution.py:677
  26.0 0.7 %copy.4 = f32[1,6,16,8,128]{4,3,2,1,0:T(8,128)} copy(f32[1,6,16,8,128]{4,3,2,1,0:T(8,128)S(1)} %bitcast.2) | data formatting | bytes 786432

commit v7 on v6

--- a/solution.py
+++ b/solution.py
@@ -20,7 +20,7 @@
 CH = 4
 NC = K // CH
 Z_COL, Z_DIFF = 2 * NC, 2 * NC + 1
-N_Z = 2 * NC + 2
+N_Z = 2 * NC + 3
 DEPTH = 4
 VIA_FIRST = 2
 VIA_SECOND = 3
@@ -218,7 +218,7 @@
     def chunk(field, c, target, relayed=False):
         part = field * K + c * CH
         slot = field * NC + c
-        src = rows_of(zm if relayed else x_hbm, part, CH)
+        src = rows_of(zm if relayed else x, part, CH)
         return remote(src, rows_of(zm, part, CH), zsend_sem.at[0 if relayed else target - 1, slot], zrecv_sem.at[slot],
                       {"sect": target})
 
@@ -226,9 +226,9 @@
         return remote(flow_cols if relayed else flow_cols_out, flow_cols, zsend_sem.at[0 if relayed else target - 1, Z_COL],
                       zrecv_sem.at[Z_COL], {"sect": target})
 
-    def send_diff(target, relayed=False):
-        part = diff.at[8:K * 8]
-        return remote(part, part, zsend_sem.at[0 if relayed else target - 1, Z_DIFF], zrecv_sem.at[Z_DIFF], {"sect": target})
+    def send_half(half, target, relayed=False):
+        part = diff.at[8:K * 4] if half else diff.at[K * 4:K * 8]
+        return remote(part, part, zsend_sem.at[0 if relayed else target - 1, Z_DIFF + half], zrecv_sem.at[Z_DIFF + half], {"sect": target})
 
     def to_tracers(act, targets, *copies):
         for target in targets:
@@ -243,6 +243,7 @@
     def wait_send(copy):
         copy.wait_send()
 
+    halves = [functools.partial(send_half, half) for half in range(2)]
     chunks = [functools.partial(chunk, field, c) for c in range(NC) for field in range(2)]
 
     await_ready(E)
@@ -278,6 +279,11 @@
         diff[0:8, :] = zero
 
     await_ready(SECOND, onward)
+
+    @pl.when(back)
+    def _():
+        send_cols(peer, True).wait_recv()
+        send_cols(peer, True).start()
 
     @pl.when(passes_on)
     def _():
@@ -416,12 +422,13 @@
                     signal(ready.at[GO], {"lon": lon + 2 * (other - MID)})
 
         pl.semaphore_wait(ready.at[GO], 1)
-        to_tracers(start, (1, 2), send_diff)
+        to_tracers(start, (1, 2), *halves)
 
         @pl.when(place == 0)
         def _():
-            send_diff(1).wait_send()
+            halves[0](1).wait_send()
             signal(ready.at[GO], {"lon": lon + 2 * MID})
+            halves[1](1).wait_send()
 
     @pl.when(sect != 0)
     def _():
@@ -486,16 +493,19 @@
         def _():
             turn_rows()
 
-        send_cols(1).wait_recv()
-
-        @pl.when(passes_on)
+        @pl.when(jnp.logical_not(back))
+        def _():
+            send_cols(1).wait_recv()
+
+        @pl.when(onward)
         def _():
             send_cols(peer, True).start()
 
         @pl.when(back)
         def _():
-            send_diff(peer, True).wait_recv()
-            send_diff(peer, True).start()
+            for make in halves:
+                make(peer, True).wait_recv()
+                make(peer, True).start()
 
 
         p1_lev = jnp.where(even, bcast(near[8:16, 62:63]), bcast(near[8:16, 63:64]))
@@ -589,11 +599,13 @@
 
         @pl.when(jnp.logical_not(back))
         def _():
-            send_diff(1).wait_recv()
+            for make in halves:
+                make(1).wait_recv()
 
         @pl.when(onward)
         def _():
-            send_diff(peer, True).start()
+            for make in halves:
+                make(peer, True).start()
 
 
         def eliminate(i, carry):
@@ -661,11 +673,11 @@
 
         @pl.when(place != 0)
         def _():
-            to_tracers(wait_send, (1, 2), send_diff)
+            to_tracers(wait_send, (1, 2), *halves)
 
     @pl.when(passes_on)
     def _():
-        for make in (*chunks, send_cols, send_diff):
+        for make in (*chunks, send_cols, *halves):
             make(peer, True).wait_send()
 
 

time: 26.9 us -> 26.6 us (0.989)
  Pallas kernels: 26 us -> 25.7 us
    pallas_call x1, Pallas kernels: 26 us -> 25.7 us  [on_device(): pl.pallas_call(functools.partial(kernel, n_sect, n_lon, n_lat), out_shape...]
where the time goes in v7:
time: 26.6 us; the launch traced here: 26.4 us
  Pallas kernels  25.7 us (97%)
  local copies, waits for them, and re-layouts  0.75 us (3%)
    pallas_call x1, Pallas kernels, on_device(): pl.pallas_call(functools.partial(kernel, n_sect, n_lon, n_lat), out_shape...  25.7 us
    unnamed x1, local copies, waits for them, and re-layouts  0.75 us

profile of v7, /device:TPU:128, one launch (start us, length us, event | category | flops | bytes accessed | tf_op | source)
XLA Modules:
  0.0 26.4 jit_solution(10848321029277948487)
XLA Ops:
  0.0 25.7 %shard_map.28 = f32[768,128]{1,0:T(8,128)S(1)} custom-call(f32[768,128]{1,0:T(8,128)} %bitcast.3, s32[8,128]{1,0:T(8,128)} %lev_hbm.1), custom_call_target="tpu_custom_call" | custom-call | tf_op jit(solution)/shard_map/pallas_call | solution.py:689
  25.7 0.7 %copy.4 = f32[1,6,16,8,128]{4,3,2,1,0:T(8,128)} copy(f32[1,6,16,8,128]{4,3,2,1,0:T(8,128)S(1)} %bitcast.2) | data formatting | bytes 786432
